TPU v7x, 32 devices: a whole 2x2x4 slice. The times are simulated.
32 devices in a mesh: wide: 16 (over z, y, core), narrow: 2 (over x).
Axes of the slice: x: 2, y: 2, z: 4, core: 2. Of those that a mesh axis runs over, the one named last changes fastest.
Arguments:
- left: bfloat16 [64, 1024, 256], P(None, 'wide', 'narrow'), may hold values from -6 to 6
- right: bfloat16 [64, 1024, 256], P(None, 'wide', 'narrow'), may hold values from -6 to 6
- bond_signs: int32 [4, 8, 1024, 256], P(None, None, 'wide', 'narrow'), may hold values from 0 to 1
- hop: float32 [4, 4], replicated, may hold values from 0.2 to 1
Outputs:
- moments: float32 [16, 64, 64], P(None, 'wide', 'narrow')
All inputs are finite; a program needn't handle non-finite values.
Results may differ from a plain program's by a relative error of at most 0.004.
Values may be sent and summed in bfloat16 or wider, within the bound.
No kernel may reach another device: no remote copies, remote signals or barrier semaphores. Data moves between devices by JAX's collectives and lax.ppermute only.
A program may use at most 64 MiB of HBM per device.

v0:
```python
import math

import jax
import jax.numpy as jnp
from jax import lax
from jax.experimental import pallas as pl
from jax.experimental.pallas import tpu as pltpu
from jax.sharding import PartitionSpec as P

OPS = 4
RANGE = 4
TAPS = 2 * RANGE
EVEN = tuple(a for a in range(OPS) if a % 2 == 0)
ODD = tuple(a for a in range(OPS) if a % 2 == 1)
SUB = 8
LANES = 128
VMEM = pltpu.VMEM
F32 = jnp.float32
BF16 = jnp.bfloat16


def lane_index(shape):
    return lax.broadcasted_iota(jnp.int32, shape, len(shape) - 1)


def pack_kernel(parity, right, left, bonds, near, far, side, head, tail):
    count, rows, cols = right.shape
    even = parity[0] == 0
    group = LANES // TAPS

    def sign_of(a, index):
        return (2 * bonds[a, index] - 1).astype(F32)

    fields = [(right, count), (left, count)]
    slot = 0
    for ref, n in fields:
        @pl.loop(0, n)
        def _(v, ref=ref, slot=slot):
            at = pl.multiple_of((v + slot) * SUB, SUB)
            head[pl.ds(at, SUB), :] = ref[v, : 2 * SUB, :].astype(F32)[:SUB]
            tail[pl.ds(at, SUB), :] = ref[v, rows - 2 * SUB :, :].astype(F32)[SUB:]

        slot += n
    for a in EVEN:
        for index in range(TAPS):
            head[slot * SUB : slot * SUB + SUB, :] = (2 * bonds[a, index, :SUB, :] - 1).astype(F32)
            tail[slot * SUB : slot * SUB + SUB, :] = (2 * bonds[a, index, rows - SUB :, :] - 1).astype(F32)
            slot += 1
    for base in range(0, slot, 2 * SUB):
        for row in range(RANGE):
            def strip(ref, offset):
                parts = [ref[pl.ds((base + half * SUB) * SUB + offset, SUB, stride=SUB), :] for half in range(2)]
                return jnp.concatenate(parts, axis=0)

            low = strip(head, row)
            high = strip(tail, SUB - RANGE + row)
            near[row, base : base + 2 * SUB, :] = jnp.where(even, high, low).astype(BF16)
            far[row, base : base + 2 * SUB, :] = jnp.where(even, low, high).astype(BF16)

    lane = lane_index((rows, cols))
    for which, ref in enumerate((right, left)):
        for block in range(count // group):
            total = jnp.zeros((rows, cols), F32)
            for t in range(group):
                moved = pltpu.roll(ref[block * group + t].astype(F32), RANGE + TAPS * t, 1)
                total = jnp.where(lane // TAPS == t, moved, total)
            side[which * (count // group) + block] = total.astype(BF16)
    total = jnp.zeros((rows, cols), F32)
    for t in range(len(ODD) * TAPS):
        moved = pltpu.roll(sign_of(ODD[t // TAPS], t % TAPS), RANGE + TAPS * t, 1)
        total = jnp.where(lane // TAPS == t, moved, total)
    side[2 * (count // group)] = total.astype(BF16)


def main_kernel(widths, parity, hop, right, left, bonds, near, far, side, out,
                value, edge, coef, turned, acc, back_a, first_a, back_b, first_b):
    count, rows, cols = right.shape
    even = parity[0] == 0
    group = LANES // TAPS
    stride = rows + 2 * SUB
    lane = lane_index((SUB, cols))
    lane_all = lane_index((rows, cols))

    def outer(slab, row):
        low = jnp.where(even, far[row, slab, :].astype(F32), near[row, slab, :].astype(F32))
        high = jnp.where(even, near[row, slab, :].astype(F32), far[row, slab, :].astype(F32))
        return low, high

    for which, ref in enumerate((right, left)):
        @pl.loop(0, count)
        def _(v, which=which, ref=ref):
            value[which, pl.ds(pl.multiple_of(v * stride + SUB, SUB), rows), :] = ref[v].astype(F32)

        for base in range(0, count, 2 * SUB):
            for row in range(RANGE):
                low, high = outer(slice(which * count + base, which * count + base + 2 * SUB), row)
                for half in range(2):
                    at = (base + half * SUB) * stride + row
                    part = slice(half * SUB, half * SUB + SUB)
                    value[which, pl.ds(at + SUB - RANGE, SUB, stride=stride), :] = low[part]
                    value[which, pl.ds(at + SUB + rows, SUB, stride=stride), :] = high[part]

        @pl.loop(0, count // group)
        def _(block, which=which):
            packed = side[which * (count // group) + block].astype(F32)
            for t in range(group):
                at = pl.multiple_of((block * group + t) * rows, SUB)
                edge[which, pl.ds(at, rows), :] = pltpu.roll(packed, (LANES - RANGE - TAPS * t) % LANES, 1)

    for a in range(OPS):
        for index in range(TAPS):
            scale = hop[a, index % RANGE] * (1.0 if index < RANGE else -1.0)
            coef[a * TAPS + index, SUB : SUB + rows, :] = (2 * bonds[a, index] - 1).astype(F32) * scale
    for row in range(RANGE):
        low, high = outer(slice(2 * count, 2 * count + 2 * SUB), row)
        for slot in range(len(EVEN) * TAPS):
            a, index = EVEN[slot // TAPS], slot % TAPS
            scale = hop[a, index % RANGE] * (1.0 if index < RANGE else -1.0)
            where = SUB - RANGE + row if index < RANGE else SUB + rows + row
            source = low if index < RANGE else high
            coef[a * TAPS + index, where : where + 1, :] = source[slot : slot + 1] * scale
    packed = side[2 * (count // group)].astype(F32)
    for slot in range(len(ODD) * TAPS):
        a, index = ODD[slot // TAPS], slot % TAPS
        step = index % RANGE + 1
        scale = hop[a, index % RANGE] * (1.0 if index < RANGE else -1.0)
        beyond = pltpu.roll(packed, (LANES - RANGE - TAPS * slot) % LANES, 1) * scale
        inside = coef[a * TAPS + index, SUB : SUB + rows, :]
        if index < RANGE:
            turned[slot] = pltpu.roll(jnp.where(lane_all >= cols - step, beyond, inside), step, 1)
        else:
            turned[slot] = pltpu.roll(jnp.where(lane_all < step, beyond, inside), cols - step, 1)

    acc[...] = jnp.zeros_like(acc)

    def stencil(row, part, back, first):
        for which, target in ((0, first), (1, back)):
            factors = {}
            for a in range(OPS):
                for index in range(TAPS):
                    step = index % RANGE + 1
                    if which == 0:
                        source, at = coef.at[a * TAPS + index], row + SUB
                    elif a % 2 == 0:
                        source, at = coef.at[a * TAPS + index], row + SUB + (-step if index < RANGE else step)
                    else:
                        source, at = turned.at[ODD.index(a) * TAPS + index], row
                    factors[a, index] = source[pl.ds(at, SUB, stride=0), :]
            ahead = 1 if which == 0 else -1
            for pair in range(count // (2 * SUB)):
                sums = {a: [] for a in range(OPS)}
                for half in range(2):
                    first_vec = (2 * pair + half) * SUB
                    here = first_vec * stride + row + SUB
                    total = {}
                    for index in range(TAPS):
                        step = (index % RANGE + 1) * (ahead if index < RANGE else -ahead)
                        moved = value[which, pl.ds(here + step, SUB, stride=stride), :]
                        for a in EVEN:
                            term = factors[a, index] * moved
                            total[a] = term if index == 0 else total[a] + term
                    middle = value[which, pl.ds(here, SUB, stride=stride), :]
                    beyond = edge[which, pl.ds(first_vec * rows + row, SUB, stride=rows), :]
                    for index in range(TAPS):
                        step = (index % RANGE + 1) * (ahead if index < RANGE else -ahead)
                        inner = (lane < step) if step > 0 else (lane >= cols + step)
                        moved = pltpu.roll(jnp.where(inner, beyond, middle), (cols - step) % cols, 1)
                        for a in ODD:
                            term = factors[a, index] * moved
                            total[a] = term if index == 0 else total[a] + term
                    for a in range(OPS):
                        sums[a].append(total[a])
                for a in range(OPS):
                    at = a * count + pair * 2 * SUB
                    target[at : at + 2 * SUB, part * cols : part * cols + cols] = jnp.concatenate(sums[a], axis=0).astype(BF16)

    def product(back, first):
        acc[...] += lax.dot_general(back[...], first[...], (((1,), (1,)), ((), ())), preferred_element_type=F32)

    back_b[...] = jnp.zeros_like(back_b)
    first_b[...] = jnp.zeros_like(first_b)

    @pl.loop(0, rows // 4)
    def _(step):
        product(back_b, first_b)
        for part in range(2):
            stencil(step * 4 + part, part, back_a, first_a)
        product(back_a, first_a)
        for part in range(2):
            stencil(step * 4 + 2 + part, part, back_b, first_b)

    product(back_b, first_b)

    parts_left, parts_right = widths
    per_left, per_right = count // parts_left, count // parts_right
    size = OPS * count

    def order(parts, per, dim):
        new = lax.broadcasted_iota(jnp.int32, (size, size), dim)
        old = lax.broadcasted_iota(jnp.int32, (size, size), 1 - dim)
        part, rest = new // (OPS * per), new % (OPS * per)
        return jnp.where(old == (rest // per) * count + part * per + rest % per, 1.0, 0.0).astype(BF16)

    moved = jnp.dot(order(parts_left, per_left, 0), acc[...].astype(BF16), preferred_element_type=F32).astype(BF16)
    moved = jnp.dot(moved, order(parts_right, per_right, 1), preferred_element_type=F32).astype(BF16)
    if out.ndim == 2:
        out[...] = moved
    else:
        width = OPS * per_right
        for d in range(parts_left * parts_right):
            w, r = divmod(d, parts_right)
            out[d] = moved[w * OPS * per_left : (w + 1) * OPS * per_left, r * width : (r + 1) * width]


def sum_kernel(factor, got, out):
    total = jnp.sum(got[...].astype(F32), axis=0) * factor
    per_left, per_right = out.shape[1], out.shape[2]
    for a in range(OPS):
        for b in range(OPS):
            out[a * OPS + b] = total[a * per_left : (a + 1) * per_left, b * per_right : (b + 1) * per_right]


def swap(array, axis, pairs):
    return lax.ppermute(array, axis, pairs)


def on_device(left, right, bond_signs, hop):
    count, rows, cols = right.shape
    wide, narrow = lax.axis_size("wide"), lax.axis_size("narrow")
    group = LANES // TAPS
    blocks = 2 * (count // group) + 1
    edge_rows = 2 * count + len(EVEN) * TAPS
    parity = (lax.axis_index("wide") % 2).astype(jnp.int32).reshape(1)
    smem = pl.BlockSpec(memory_space=pltpu.SMEM)
    vmem = pl.BlockSpec(memory_space=pltpu.VMEM)

    near, far, side = pl.pallas_call(
        pack_kernel,
        out_shape=(
            jax.ShapeDtypeStruct((RANGE, edge_rows, cols), BF16),
            jax.ShapeDtypeStruct((RANGE, edge_rows, cols), BF16),
            jax.ShapeDtypeStruct((blocks, rows, cols), BF16),
        ),
        in_specs=[smem, vmem, vmem, vmem],
        out_specs=(vmem, vmem, vmem),
        scratch_shapes=[VMEM((edge_rows * SUB, cols), F32), VMEM((edge_rows * SUB, cols), F32)],
        name="pack",
    )(parity, right, left, bond_signs)

    far = swap(far, "wide", [(i, (i + 1) % wide if i % 2 else (i - 1) % wide) for i in range(wide)])
    near = swap(near, "wide", [(i, i ^ 1) for i in range(wide)])
    if narrow == 2:
        side = swap(side, "narrow", [(0, 1), (1, 0)])
    else:
        before = swap(side, "narrow", [(i, (i + 1) % narrow) for i in range(narrow)])
        after = swap(side, "narrow", [((i + 1) % narrow, i) for i in range(narrow)])
        side = jnp.where(lane_index(side.shape) % TAPS < RANGE, before, after)

    per_left, per_right = count // wide, count // narrow
    size = OPS * count
    direct = (OPS * per_right) % LANES == 0 and (OPS * per_left) % 16 == 0
    blocked = (wide * narrow, OPS * per_left, OPS * per_right)
    partial = pl.pallas_call(
        lambda *refs: main_kernel((wide, narrow), *refs),
        out_shape=jax.ShapeDtypeStruct(blocked if direct else (size, size), BF16),
        in_specs=[smem, smem] + [vmem] * 6,
        out_specs=vmem,
        scratch_shapes=[
            VMEM((2, count * (rows + 2 * SUB), cols), F32),
            VMEM((2, count * rows, cols), F32),
            VMEM((OPS * TAPS, rows + 2 * SUB, cols), F32),
            VMEM((len(ODD) * TAPS, rows, cols), F32),
            VMEM((size, size), F32),
        ] + [VMEM((size, 2 * cols), BF16)] * 4,
        name="moments",
    )(parity, hop, right, left, bond_signs, near, far, side)
    if not direct:
        partial = partial.reshape(wide, OPS * per_left, narrow, OPS * per_right).transpose(0, 2, 1, 3).reshape(blocked)
    got = lax.all_to_all(partial, ("wide", "narrow"), 0, 0, tiled=True)
    factor = 1.0 / math.sqrt(rows * cols * wide * narrow)
    return pl.pallas_call(
        lambda *refs: sum_kernel(factor, *refs),
        out_shape=jax.ShapeDtypeStruct((OPS * OPS, per_left, per_right), F32),
        in_specs=[vmem],
        out_specs=vmem,
        name="total",
    )(got)


def solution(mesh):
    in_specs = (
        P(None, "wide", "narrow"),
        P(None, "wide", "narrow"),
        P(None, None, "wide", "narrow"),
        P(),
    )
    out_specs = P(None, "wide", "narrow")
    return jax.shard_map(
        on_device, mesh=mesh, in_specs=in_specs, out_specs=out_specs, check_vma=False
    )
```

profile of v0, /device:TPU:0, one launch (start us, length us, event | category | flops | bytes accessed | tf_op | source)
XLA Modules:
  0.0 56.5 jit_solution(358004106156858862)
XLA Ops:
  0.0 4.2 %pack.1 = (bf16[4,144,128]{2,1,0:T(8,128)(2,1)}, bf16[4,144,128]{2,1,0:T(8,128)(2,1)}, bf16[9,64,128]{2,1,0:T(8,128)(2,1)}) custom-call(s32[1]{0:T(128)} %bitcast.parity.refs_0_, bf16[64,64,128]{2,1,0:T(8,128)(2,1)} %refs_2_.1, bf16[64,64,128]{2,1,0:T(8,128)(2,1)} %refs_3_.1, s32[4,8,64,128]{3,2,1,0:T(8,128)} %refs_4_.1), custom_call_target="tpu_custom_call" | custom-call | tf_op jit(solution)/shard_map/pack/pallas_call | solution.py:237
  4.2 0.5 collective-permute-start
  4.7 5.7 %collective-permute-start.1 = (bf16[4,144,128]{2,1,0:T(8,128)(2,1)}, bf16[4,144,128]{2,1,0:T(8,128)(2,1)S(1)}, u32[]{:S(2)}, u32[]{:S(2)}) collective-permute-start(bf16[4,144,128]{2,1,0:T(8,128)(2,1)} %get-tuple-element.9), channel_id=1, source_target_pairs={{0,30},{2,4},{4,2},{6,8},{8,6},{10,12},{12,10},{14,16},{16,14},{18... | collective-permute-start | bytes 442376 | tf_op jit(solution)/shard_map/ppermute | solution.py:224
  10.3 1.5 %collective-permute-start.2 = (bf16[9,64,128]{2,1,0:T(8,128)(2,1)}, bf16[9,64,128]{2,1,0:T(8,128)(2,1)S(1)}, u32[]{:S(2)}, u32[]{:S(2)}) collective-permute-start(bf16[9,64,128]{2,1,0:T(8,128)(2,1)} %get-tuple-element.10), channel_id=1, source_target_pairs={{0,1},{1,0},{2,3},{3,2},{4,5},{5,4},{6,7},{7,6},{8,9},{9,8},{10,11... | collective-permute-start | bytes 442376 | tf_op jit(solution)/shard_map/ppermute | solution.py:224
  11.8 0.0 collective-permute-done.refs_5_
  11.8 0.0 copy-start
  11.8 1.5 %collective-permute-done.1.refs_6_ = bf16[4,144,128]{2,1,0:T(8,128)(2,1)S(1)} collective-permute-done((bf16[4,144,128]{2,1,0:T(8,128)(2,1)}, bf16[4,144,128]{2,1,0:T(8,128)(2,1)S(1)}, u32[]{:S(2)}, u32[]{:S(2)}) %collective-permute-start.1) | collective-permute-done | bytes 147488 | tf_op jit(solution)/shard_map/ppermute | solution.py:224
  13.4 0.0 copy-start.1
  13.4 2.3 %collective-permute-done.2.refs_7_ = bf16[9,64,128]{2,1,0:T(8,128)(2,1)S(1)} collective-permute-done((bf16[9,64,128]{2,1,0:T(8,128)(2,1)}, bf16[9,64,128]{2,1,0:T(8,128)(2,1)S(1)}, u32[]{:S(2)}, u32[]{:S(2)}) %collective-permute-start.2) | collective-permute-done | bytes 147488 | tf_op jit(solution)/shard_map/ppermute | solution.py:224
  15.7 0.0 copy-done
  15.7 0.0 copy-done.1
  15.7 0.0 copy-start.2
  15.7 0.7 %copy-done.2 = bf16[9,64,128]{2,1,0:T(8,128)(2,1)} copy-done((bf16[9,64,128]{2,1,0:T(8,128)(2,1)}, bf16[9,64,128]{2,1,0:T(8,128)(2,1)S(1)}, u32[]{:S(2)}) %copy-start.2) | copy-done | bytes 147480
  16.3 25.8 %moments.1 = bf16[32,16,128]{2,1,0:T(8,128)(2,1)} custom-call(s32[1]{0:T(128)} %bitcast.parity.refs_0_, f32[4,4]{1,0:T(4,128)} %refs_1_.1, bf16[64,64,128]{2,1,0:T(8,128)(2,1)} %refs_2_.1, bf16[64,64,128]{2,1,0:T(8,128)(2,1)} %refs_3_.1, s32[4,8,64,128]{3,2,1,0:T(8,128)} %refs_4_.1, bf16[4,144,128]{2,1,0:T(8,128)(2,1)} %copy-done, ...), custom_call_target="tpu_custom_call" | custom-call | tf_op jit(solution)/shard_map/moments/pallas_call | solution.py:263
  42.1 12.8 %all_to_all.5.refs_0_ = bf16[32,16,128]{2,1,0:T(8,128)(2,1)} all-to-all(bf16[32,16,128]{2,1,0:T(8,128)(2,1)} %moments.1), channel_id=1, replica_groups=mesh['wide'=16,'narrow'=2] {'wide','narrow'}, dimensions={0} | all-to-all | bytes 262144 | tf_op jit(solution)/shard_map/all_to_all | solution.py:279
  54.9 1.6 %total.1 = f32[16,4,32]{2,1,0:T(4,128)} custom-call(bf16[32,16,128]{2,1,0:T(8,128)(2,1)} %all_to_all.5.refs_0_), custom_call_target="tpu_custom_call" | custom-call | tf_op jit(solution)/shard_map/total/pallas_call | solution.py:281
Async XLA Ops:
  4.2 7.6 %collective-permute-start = (bf16[4,144,128]{2,1,0:T(8,128)(2,1)}, bf16[4,144,128]{2,1,0:T(8,128)(2,1)S(1)}, u32[]{:S(2)}, u32[]{:S(2)}) collective-permute-start(bf16[4,144,128]{2,1,0:T(8,128)(2,1)} %get-tuple-element.8), channel_id=1, source_target_pairs={{0,2},{2,0},{4,6},{6,4},{8,10},{10,8},{12,14},{14,12},{16,18},{18,... | collective-permute-start | bytes 442376 | tf_op jit(solution)/shard_map/ppermute | solution.py:224
  4.7 8.7 %collective-permute-start.1 = (bf16[4,144,128]{2,1,0:T(8,128)(2,1)}, bf16[4,144,128]{2,1,0:T(8,128)(2,1)S(1)}, u32[]{:S(2)}, u32[]{:S(2)}) collective-permute-start(bf16[4,144,128]{2,1,0:T(8,128)(2,1)} %get-tuple-element.9), channel_id=1, source_target_pairs={{0,30},{2,4},{4,2},{6,8},{8,6},{10,12},{12,10},{14,16},{16,14},{18... | collective-permute-start | bytes 442376 | tf_op jit(solution)/shard_map/ppermute | solution.py:224
  10.3 5.4 %collective-permute-start.2 = (bf16[9,64,128]{2,1,0:T(8,128)(2,1)}, bf16[9,64,128]{2,1,0:T(8,128)(2,1)S(1)}, u32[]{:S(2)}, u32[]{:S(2)}) collective-permute-start(bf16[9,64,128]{2,1,0:T(8,128)(2,1)} %get-tuple-element.10), channel_id=1, source_target_pairs={{0,1},{1,0},{2,3},{3,2},{4,5},{5,4},{6,7},{7,6},{8,9},{9,8},{10,11... | collective-permute-start | bytes 442376 | tf_op jit(solution)/shard_map/ppermute | solution.py:224
  11.8 3.9 %copy-start = (bf16[4,144,128]{2,1,0:T(8,128)(2,1)}, bf16[4,144,128]{2,1,0:T(8,128)(2,1)S(1)}, u32[]{:S(2)}) copy-start(bf16[4,144,128]{2,1,0:T(8,128)(2,1)S(1)} %collective-permute-done.refs_5_) | copy-start | bytes 442372
  13.4 2.3 %copy-start.1 = (bf16[4,144,128]{2,1,0:T(8,128)(2,1)}, bf16[4,144,128]{2,1,0:T(8,128)(2,1)S(1)}, u32[]{:S(2)}) copy-start(bf16[4,144,128]{2,1,0:T(8,128)(2,1)S(1)} %collective-permute-done.1.refs_6_) | copy-start | bytes 442372
  15.7 0.7 %copy-start.2 = (bf16[9,64,128]{2,1,0:T(8,128)(2,1)}, bf16[9,64,128]{2,1,0:T(8,128)(2,1)S(1)}, u32[]{:S(2)}) copy-start(bf16[9,64,128]{2,1,0:T(8,128)(2,1)S(1)} %collective-permute-done.2.refs_7_) | copy-start | bytes 442372
where the time goes:
time: 56.7 us; the launch traced here: 56.5 us
  Pallas kernels  31.6 us (56%)
  blocking collectives  12.8 us (23%)
  starting transfers between devices  7.64 us (13%)
  waiting for transfers between devices  3.86 us (7%)
  local copies, waits for them, and re-layouts  0.67 us (1%)
    pallas_call x1, Pallas kernels, on_device(): pl.pallas_call(lambda *refs: main_kernel((wide, narrow), *refs), out_shap...  25.8 us
    all_to_all x1, blocking collectives, on_device(): got = lax.all_to_all(partial, ('wide', 'narrow'), 0, 0, tiled=True)  12.8 us
    ppermute x3, starting transfers between devices, swap(): return lax.ppermute(array, axis, pairs)  7.64 us
    pallas_call x1, Pallas kernels, on_device(): pl.pallas_call(pack_kernel, out_shape=(jax.ShapeDtypeStruct((RANGE, edge_...  4.18 us
    ppermute x3, waiting for transfers between devices, swap(): return lax.ppermute(array, axis, pairs)  3.86 us
    pallas_call x1, Pallas kernels, on_device(): pl.pallas_call(lambda *refs: sum_kernel(factor, *refs), out_shape=jax.Sha...  1.63 us
  transfers between devices with their start and end apart: 3, of which 2 were waited for; matrix products, arithmetic and copies ran while one was open for 0% of the time, Pallas kernels for 0%

commit v1 on v0

--- a/solution.py
+++ b/solution.py
@@ -73,23 +73,78 @@
 
 
 def main_kernel(widths, parity, hop, right, left, bonds, near, far, side, out,
-                value, edge, coef, turned, acc, back_a, first_a, back_b, first_b):
+                value, rim, coef, band, mats, acc, back_a, first_a, back_b, first_b):
     count, rows, cols = right.shape
     even = parity[0] == 0
     group = LANES // TAPS
-    stride = rows + 2 * SUB
-    lane = lane_index((SUB, cols))
+    blocks = count // group
+    stride = rows + 2 * SUB + 1
+    period = 2 * TAPS
     lane_all = lane_index((rows, cols))
+
+    def scale_of(a, index):
+        return hop[a, index % RANGE] * (1.0 if index < RANGE else -1.0)
 
     def outer(slab, row):
         low = jnp.where(even, far[row, slab, :].astype(F32), near[row, slab, :].astype(F32))
         high = jnp.where(even, near[row, slab, :].astype(F32), far[row, slab, :].astype(F32))
         return low, high
 
-    for which, ref in enumerate((right, left)):
-        @pl.loop(0, count)
-        def _(v, which=which, ref=ref):
-            value[which, pl.ds(pl.multiple_of(v * stride + SUB, SUB), rows), :] = ref[v].astype(F32)
+    for a in range(OPS):
+        for index in range(TAPS):
+            coef[a * TAPS + index, SUB : SUB + rows, :] = (2 * bonds[a, index] - 1).astype(F32) * scale_of(a, index)
+    for row in range(RANGE):
+        low, high = outer(slice(2 * count, 2 * count + 2 * SUB), row)
+        for slot in range(len(EVEN) * TAPS):
+            a, index = EVEN[slot // TAPS], slot % TAPS
+            where = SUB - RANGE + row if index < RANGE else SUB + rows + row
+            source = low if index < RANGE else high
+            coef[a * TAPS + index, where : where + 1, :] = source[slot : slot + 1] * scale_of(a, index)
+
+    inner_lane = lane_all % TAPS
+    last = inner_lane < RANGE
+    signs = side[2 * blocks].astype(F32)
+    weights = {}
+    for which in range(2):
+        for a in ODD:
+            for k in range(1, RANGE + 1):
+                if which == 0:
+                    tops = pltpu.roll(coef[a * TAPS + k - 1, SUB : SUB + rows, :], RANGE, 1)
+                    bottoms = pltpu.roll(coef[a * TAPS + RANGE + k - 1, SUB : SUB + rows, :], RANGE, 1)
+                else:
+                    slot = ODD.index(a) * TAPS + k - 1
+                    bottoms = pltpu.roll(signs, (k - TAPS * slot) % LANES, 1) * scale_of(a, k - 1)
+                    tops = pltpu.roll(signs, (-k - TAPS * (slot + RANGE)) % LANES, 1) * scale_of(a, RANGE + k - 1)
+                one = jnp.where(lane_all < RANGE, tops, bottoms)
+                valid = ((lane_all < RANGE) & (lane_all + k >= RANGE)) | ((lane_all >= RANGE) & (lane_all - k < RANGE) & (lane_all < TAPS))
+                one = jnp.where(valid, one, 0.0)
+                for shift in (TAPS, 2 * TAPS, 4 * TAPS, 8 * TAPS):
+                    one = one + pltpu.roll(one, shift, 1)
+                weights[which, a, k] = one
+        for block in range(blocks):
+            packed = side[which * blocks + block].astype(F32)
+            total = {}
+            for k in range(1, RANGE + 1):
+                moved = jnp.where(last, pltpu.roll(packed, LANES - k, 1), pltpu.roll(packed, k, 1))
+                for a in ODD:
+                    term = weights[which, a, k] * moved
+                    total[a] = term if k == 1 else total[a] + term
+            for a in ODD:
+                band[which * blocks + block, ODD.index(a)] = total[a]
+
+        ref = (right, left)[which]
+
+        @pl.loop(0, blocks)
+        def _(block, which=which, ref=ref):
+            for o in range(len(ODD)):
+                packed = band[which * blocks + block, o]
+                for t in range(group):
+                    moved = pltpu.roll(packed, (LANES - RANGE - TAPS * t) % LANES, 1)
+                    moved = jnp.where((lane_all < RANGE) | (lane_all >= cols - RANGE), moved, 0.0)
+                    rim[which, o, pl.ds((block * group + t) * (rows + 1), rows), :] = moved
+            for t in range(group):
+                v = block * group + t
+                value[which, pl.ds(v * stride + SUB, rows), :] = ref[v].astype(F32)
 
         for base in range(0, count, 2 * SUB):
             for row in range(RANGE):
@@ -100,58 +155,54 @@
                     value[which, pl.ds(at + SUB - RANGE, SUB, stride=stride), :] = low[part]
                     value[which, pl.ds(at + SUB + rows, SUB, stride=stride), :] = high[part]
 
-        @pl.loop(0, count // group)
-        def _(block, which=which):
-            packed = side[which * (count // group) + block].astype(F32)
-            for t in range(group):
-                at = pl.multiple_of((block * group + t) * rows, SUB)
-                edge[which, pl.ds(at, rows), :] = pltpu.roll(packed, (LANES - RANGE - TAPS * t) % LANES, 1)
-
-    for a in range(OPS):
-        for index in range(TAPS):
-            scale = hop[a, index % RANGE] * (1.0 if index < RANGE else -1.0)
-            coef[a * TAPS + index, SUB : SUB + rows, :] = (2 * bonds[a, index] - 1).astype(F32) * scale
-    for row in range(RANGE):
-        low, high = outer(slice(2 * count, 2 * count + 2 * SUB), row)
-        for slot in range(len(EVEN) * TAPS):
-            a, index = EVEN[slot // TAPS], slot % TAPS
-            scale = hop[a, index % RANGE] * (1.0 if index < RANGE else -1.0)
-            where = SUB - RANGE + row if index < RANGE else SUB + rows + row
-            source = low if index < RANGE else high
-            coef[a * TAPS + index, where : where + 1, :] = source[slot : slot + 1] * scale
-    packed = side[2 * (count // group)].astype(F32)
-    for slot in range(len(ODD) * TAPS):
-        a, index = ODD[slot // TAPS], slot % TAPS
-        step = index % RANGE + 1
-        scale = hop[a, index % RANGE] * (1.0 if index < RANGE else -1.0)
-        beyond = pltpu.roll(packed, (LANES - RANGE - TAPS * slot) % LANES, 1) * scale
-        inside = coef[a * TAPS + index, SUB : SUB + rows, :]
-        if index < RANGE:
-            turned[slot] = pltpu.roll(jnp.where(lane_all >= cols - step, beyond, inside), step, 1)
-        else:
-            turned[slot] = pltpu.roll(jnp.where(lane_all < step, beyond, inside), cols - step, 1)
-
     acc[...] = jnp.zeros_like(acc)
 
-    def stencil(row, part, back, first):
+    tile = (period, cols)
+    gap = (lane_index(tile) - lax.broadcasted_iota(jnp.int32, tile, 0)) % period
+    near_diagonal = lane_index((cols, cols)) - lax.broadcasted_iota(jnp.int32, (cols, cols), 0)
+    within = jnp.where((near_diagonal >= -TAPS) & (near_diagonal < TAPS), 1.0, 0.0).astype(BF16)
+
+    def matrices(row, slot):
+        for a in ODD:
+            total = jnp.zeros(tile, F32)
+            for k in range(1, RANGE + 1):
+                total = jnp.where(gap == period - k, coef[a * TAPS + k - 1, pl.ds(row + SUB, period, stride=0), :], total)
+                total = jnp.where(gap == k, coef[a * TAPS + RANGE + k - 1, pl.ds(row + SUB, period, stride=0), :], total)
+            high = total.astype(BF16)
+            low = (total - high.astype(F32)).astype(BF16)
+            o = ODD.index(a)
+            for part, piece in enumerate((high, low)):
+                mats[slot, part * cols : (part + 1) * cols, o * cols : (o + 1) * cols] = (
+                    jnp.concatenate([piece] * (cols // period), axis=0) * within
+                )
+
+    def stencil(row, part, slot, back, first):
+        matrices(row, slot)
+        here_lanes = slice(part * cols, (part + 1) * cols)
         for which, target in ((0, first), (1, back)):
+            middle = jnp.concatenate(
+                [value[which, pl.ds(g * SUB * stride + row + SUB, SUB, stride=stride), :] for g in range(count // SUB)], axis=0
+            ).astype(BF16)
+            for o, a in enumerate(ODD):
+                mine = slice(o * cols, (o + 1) * cols)
+                dims = (((1,), (which,)), ((), ()))
+                total = lax.dot_general(middle, mats[slot, :cols, mine], dims, preferred_element_type=F32)
+                total = total + lax.dot_general(middle, mats[slot, cols:, mine], dims, preferred_element_type=F32)
+                beyond = jnp.concatenate(
+                    [rim[which, o, pl.ds(g * SUB * (rows + 1) + row, SUB, stride=rows + 1), :] for g in range(count // SUB)], axis=0
+                )
+                target[a * count : (a + 1) * count, here_lanes] = (total + beyond).astype(BF16)
             factors = {}
-            for a in range(OPS):
+            for a in EVEN:
                 for index in range(TAPS):
                     step = index % RANGE + 1
-                    if which == 0:
-                        source, at = coef.at[a * TAPS + index], row + SUB
-                    elif a % 2 == 0:
-                        source, at = coef.at[a * TAPS + index], row + SUB + (-step if index < RANGE else step)
-                    else:
-                        source, at = turned.at[ODD.index(a) * TAPS + index], row
-                    factors[a, index] = source[pl.ds(at, SUB, stride=0), :]
+                    at = row + SUB if which == 0 else row + SUB + (-step if index < RANGE else step)
+                    factors[a, index] = coef[a * TAPS + index, pl.ds(at, SUB, stride=0), :]
             ahead = 1 if which == 0 else -1
             for pair in range(count // (2 * SUB)):
-                sums = {a: [] for a in range(OPS)}
+                sums = {a: [] for a in EVEN}
                 for half in range(2):
-                    first_vec = (2 * pair + half) * SUB
-                    here = first_vec * stride + row + SUB
+                    here = (2 * pair + half) * SUB * stride + row + SUB
                     total = {}
                     for index in range(TAPS):
                         step = (index % RANGE + 1) * (ahead if index < RANGE else -ahead)
@@ -159,20 +210,11 @@
                         for a in EVEN:
                             term = factors[a, index] * moved
                             total[a] = term if index == 0 else total[a] + term
-                    middle = value[which, pl.ds(here, SUB, stride=stride), :]
-                    beyond = edge[which, pl.ds(first_vec * rows + row, SUB, stride=rows), :]
-                    for index in range(TAPS):
-                        step = (index % RANGE + 1) * (ahead if index < RANGE else -ahead)
-                        inner = (lane < step) if step > 0 else (lane >= cols + step)
-                        moved = pltpu.roll(jnp.where(inner, beyond, middle), (cols - step) % cols, 1)
-                        for a in ODD:
-                            term = factors[a, index] * moved
-                            total[a] = term if index == 0 else total[a] + term
-                    for a in range(OPS):
+                    for a in EVEN:
                         sums[a].append(total[a])
-                for a in range(OPS):
+                for a in EVEN:
                     at = a * count + pair * 2 * SUB
-                    target[at : at + 2 * SUB, part * cols : part * cols + cols] = jnp.concatenate(sums[a], axis=0).astype(BF16)
+                    target[at : at + 2 * SUB, here_lanes] = jnp.concatenate(sums[a], axis=0).astype(BF16)
 
     def product(back, first):
         acc[...] += lax.dot_general(back[...], first[...], (((1,), (1,)), ((), ())), preferred_element_type=F32)
@@ -184,10 +226,10 @@
     def _(step):
         product(back_b, first_b)
         for part in range(2):
-            stencil(step * 4 + part, part, back_a, first_a)
+            stencil(step * 4 + part, part, part, back_a, first_a)
         product(back_a, first_a)
         for part in range(2):
-            stencil(step * 4 + 2 + part, part, back_b, first_b)
+            stencil(step * 4 + 2 + part, part, 2 + part, back_b, first_b)
 
     product(back_b, first_b)
 
@@ -266,10 +308,11 @@
         in_specs=[smem, smem] + [vmem] * 6,
         out_specs=vmem,
         scratch_shapes=[
-            VMEM((2, count * (rows + 2 * SUB), cols), F32),
-            VMEM((2, count * rows, cols), F32),
+            VMEM((2, count * (rows + 2 * SUB + 1) + SUB, cols), F32),
+            VMEM((2, len(ODD), count * (rows + 1) + SUB, cols), F32),
             VMEM((OPS * TAPS, rows + 2 * SUB, cols), F32),
-            VMEM((len(ODD) * TAPS, rows, cols), F32),
+            VMEM((blocks - 1, len(ODD), rows, cols), F32),
+            VMEM((4, 2 * cols, len(ODD) * cols), BF16),
             VMEM((size, size), F32),
         ] + [VMEM((size, 2 * cols), BF16)] * 4,
         name="moments",

time: 56.7 us -> 52.9 us (0.933)
  Pallas kernels: 31.6 us -> 27.8 us
    pallas_call x1, Pallas kernels: 25.8 us -> 22 us  [on_device(): pl.pallas_call(lambda *refs: main_kernel((wide, narrow), *refs), out_shap...]
where the time goes in v1:
time: 52.9 us; the launch traced here: 52.7 us
  Pallas kernels  27.8 us (53%)
  blocking collectives  12.8 us (24%)
  starting transfers between devices  7.64 us (14%)
  waiting for transfers between devices  3.86 us (7%)
  local copies, waits for them, and re-layouts  0.67 us (1%)
    pallas_call x1, Pallas kernels, on_device(): pl.pallas_call(lambda *refs: main_kernel((wide, narrow), *refs), out_shap...  22 us
    all_to_all x1, blocking collectives, on_device(): got = lax.all_to_all(partial, ('wide', 'narrow'), 0, 0, tiled=True)  12.8 us
    ppermute x3, starting transfers between devices, swap(): return lax.ppermute(array, axis, pairs)  7.64 us
    pallas_call x1, Pallas kernels, on_device(): pl.pallas_call(pack_kernel, out_shape=(jax.ShapeDtypeStruct((RANGE, edge_...  4.18 us
    ppermute x3, waiting for transfers between devices, swap(): return lax.ppermute(array, axis, pairs)  3.86 us
    pallas_call x1, Pallas kernels, on_device(): pl.pallas_call(lambda *refs: sum_kernel(factor, *refs), out_shape=jax.Sha...  1.63 us
  transfers between devices with their start and end apart: 3, of which 2 were waited for; matrix products, arithmetic and copies ran while one was open for 0% of the time, Pallas kernels for 0%

profile of v1, /device:TPU:0, one launch (start us, length us, event | category | flops | bytes accessed | tf_op | source)
XLA Modules:
  0.0 52.7 jit_solution(13768853231318447764)
XLA Ops:
  0.0 4.2 %pack.1 = (bf16[4,144,128]{2,1,0:T(8,128)(2,1)}, bf16[4,144,128]{2,1,0:T(8,128)(2,1)}, bf16[9,64,128]{2,1,0:T(8,128)(2,1)}) custom-call(s32[1]{0:T(128)} %bitcast.parity.refs_0_, bf16[64,64,128]{2,1,0:T(8,128)(2,1)} %refs_2_.1, bf16[64,64,128]{2,1,0:T(8,128)(2,1)} %refs_3_.1, s32[4,8,64,128]{3,2,1,0:T(8,128)} %refs_4_.1), custom_call_target="tpu_custom_call" | custom-call | tf_op jit(solution)/shard_map/pack/pallas_call | solution.py:279
  4.2 0.5 collective-permute-start
  4.7 5.7 %collective-permute-start.1 = (bf16[4,144,128]{2,1,0:T(8,128)(2,1)}, bf16[4,144,128]{2,1,0:T(8,128)(2,1)S(1)}, u32[]{:S(2)}, u32[]{:S(2)}) collective-permute-start(bf16[4,144,128]{2,1,0:T(8,128)(2,1)} %get-tuple-element.9), channel_id=1, source_target_pairs={{0,30},{2,4},{4,2},{6,8},{8,6},{10,12},{12,10},{14,16},{16,14},{18... | collective-permute-start | bytes 442376 | tf_op jit(solution)/shard_map/ppermute | solution.py:266
  10.3 1.5 %collective-permute-start.2 = (bf16[9,64,128]{2,1,0:T(8,128)(2,1)}, bf16[9,64,128]{2,1,0:T(8,128)(2,1)S(1)}, u32[]{:S(2)}, u32[]{:S(2)}) collective-permute-start(bf16[9,64,128]{2,1,0:T(8,128)(2,1)} %get-tuple-element.10), channel_id=1, source_target_pairs={{0,1},{1,0},{2,3},{3,2},{4,5},{5,4},{6,7},{7,6},{8,9},{9,8},{10,11... | collective-permute-start | bytes 442376 | tf_op jit(solution)/shard_map/ppermute | solution.py:266
  11.8 0.0 collective-permute-done.refs_5_
  11.8 0.0 copy-start
  11.8 1.5 %collective-permute-done.1.refs_6_ = bf16[4,144,128]{2,1,0:T(8,128)(2,1)S(1)} collective-permute-done((bf16[4,144,128]{2,1,0:T(8,128)(2,1)}, bf16[4,144,128]{2,1,0:T(8,128)(2,1)S(1)}, u32[]{:S(2)}, u32[]{:S(2)}) %collective-permute-start.1) | collective-permute-done | bytes 147488 | tf_op jit(solution)/shard_map/ppermute | solution.py:266
  13.4 0.0 copy-start.1
  13.4 2.3 %collective-permute-done.2.refs_7_ = bf16[9,64,128]{2,1,0:T(8,128)(2,1)S(1)} collective-permute-done((bf16[9,64,128]{2,1,0:T(8,128)(2,1)}, bf16[9,64,128]{2,1,0:T(8,128)(2,1)S(1)}, u32[]{:S(2)}, u32[]{:S(2)}) %collective-permute-start.2) | collective-permute-done | bytes 147488 | tf_op jit(solution)/shard_map/ppermute | solution.py:266
  15.7 0.0 copy-done
  15.7 0.0 copy-done.1
  15.7 0.0 copy-start.2
  15.7 0.7 %copy-done.2 = bf16[9,64,128]{2,1,0:T(8,128)(2,1)} copy-done((bf16[9,64,128]{2,1,0:T(8,128)(2,1)}, bf16[9,64,128]{2,1,0:T(8,128)(2,1)S(1)}, u32[]{:S(2)}) %copy-start.2) | copy-done | bytes 147480
  16.3 22.0 %moments.1 = bf16[32,16,128]{2,1,0:T(8,128)(2,1)} custom-call(s32[1]{0:T(128)} %bitcast.parity.refs_0_, f32[4,4]{1,0:T(4,128)} %refs_1_.1, bf16[64,64,128]{2,1,0:T(8,128)(2,1)} %refs_2_.1, bf16[64,64,128]{2,1,0:T(8,128)(2,1)} %refs_3_.1, s32[4,8,64,128]{3,2,1,0:T(8,128)} %refs_4_.1, bf16[4,144,128]{2,1,0:T(8,128)(2,1)} %copy-done, ...), custom_call_target="tpu_custom_call" | custom-call | tf_op jit(solution)/shard_map/moments/pallas_call | solution.py:305
  38.3 12.8 %all_to_all.5.refs_0_ = bf16[32,16,128]{2,1,0:T(8,128)(2,1)} all-to-all(bf16[32,16,128]{2,1,0:T(8,128)(2,1)} %moments.1), channel_id=1, replica_groups=mesh['wide'=16,'narrow'=2] {'wide','narrow'}, dimensions={0} | all-to-all | bytes 262144 | tf_op jit(solution)/shard_map/all_to_all | solution.py:322
  51.1 1.6 %total.1 = f32[16,4,32]{2,1,0:T(4,128)} custom-call(bf16[32,16,128]{2,1,0:T(8,128)(2,1)} %all_to_all.5.refs_0_), custom_call_target="tpu_custom_call" | custom-call | tf_op jit(solution)/shard_map/total/pallas_call | solution.py:324
Async XLA Ops:
  4.2 7.6 %collective-permute-start = (bf16[4,144,128]{2,1,0:T(8,128)(2,1)}, bf16[4,144,128]{2,1,0:T(8,128)(2,1)S(1)}, u32[]{:S(2)}, u32[]{:S(2)}) collective-permute-start(bf16[4,144,128]{2,1,0:T(8,128)(2,1)} %get-tuple-element.8), channel_id=1, source_target_pairs={{0,2},{2,0},{4,6},{6,4},{8,10},{10,8},{12,14},{14,12},{16,18},{18,... | collective-permute-start | bytes 442376 | tf_op jit(solution)/shard_map/ppermute | solution.py:266
  4.7 8.7 %collective-permute-start.1 = (bf16[4,144,128]{2,1,0:T(8,128)(2,1)}, bf16[4,144,128]{2,1,0:T(8,128)(2,1)S(1)}, u32[]{:S(2)}, u32[]{:S(2)}) collective-permute-start(bf16[4,144,128]{2,1,0:T(8,128)(2,1)} %get-tuple-element.9), channel_id=1, source_target_pairs={{0,30},{2,4},{4,2},{6,8},{8,6},{10,12},{12,10},{14,16},{16,14},{18... | collective-permute-start | bytes 442376 | tf_op jit(solution)/shard_map/ppermute | solution.py:266
  10.3 5.4 %collective-permute-start.2 = (bf16[9,64,128]{2,1,0:T(8,128)(2,1)}, bf16[9,64,128]{2,1,0:T(8,128)(2,1)S(1)}, u32[]{:S(2)}, u32[]{:S(2)}) collective-permute-start(bf16[9,64,128]{2,1,0:T(8,128)(2,1)} %get-tuple-element.10), channel_id=1, source_target_pairs={{0,1},{1,0},{2,3},{3,2},{4,5},{5,4},{6,7},{7,6},{8,9},{9,8},{10,11... | collective-permute-start | bytes 442376 | tf_op jit(solution)/shard_map/ppermute | solution.py:266
  11.8 3.9 %copy-start = (bf16[4,144,128]{2,1,0:T(8,128)(2,1)}, bf16[4,144,128]{2,1,0:T(8,128)(2,1)S(1)}, u32[]{:S(2)}) copy-start(bf16[4,144,128]{2,1,0:T(8,128)(2,1)S(1)} %collective-permute-done.refs_5_) | copy-start | bytes 442372
  13.4 2.3 %copy-start.1 = (bf16[4,144,128]{2,1,0:T(8,128)(2,1)}, bf16[4,144,128]{2,1,0:T(8,128)(2,1)S(1)}, u32[]{:S(2)}) copy-start(bf16[4,144,128]{2,1,0:T(8,128)(2,1)S(1)} %collective-permute-done.1.refs_6_) | copy-start | bytes 442372
  15.7 0.7 %copy-start.2 = (bf16[9,64,128]{2,1,0:T(8,128)(2,1)}, bf16[9,64,128]{2,1,0:T(8,128)(2,1)S(1)}, u32[]{:S(2)}) copy-start(bf16[9,64,128]{2,1,0:T(8,128)(2,1)S(1)} %collective-permute-done.2.refs_7_) | copy-start | bytes 442372

commit v2 on v1

--- a/solution.py
+++ b/solution.py
@@ -17,23 +17,19 @@
 VMEM = pltpu.VMEM
 F32 = jnp.float32
 BF16 = jnp.bfloat16
+VMEM_LIMIT = 24 * 1024 * 1024
 
 
 def lane_index(shape):
     return lax.broadcasted_iota(jnp.int32, shape, len(shape) - 1)
 
 
-def pack_kernel(parity, right, left, bonds, near, far, side, head, tail):
+def rows_kernel(parity, right, left, bonds, near, far, head, tail):
     count, rows, cols = right.shape
     even = parity[0] == 0
-    group = LANES // TAPS
-
-    def sign_of(a, index):
-        return (2 * bonds[a, index] - 1).astype(F32)
-
-    fields = [(right, count), (left, count)]
+
     slot = 0
-    for ref, n in fields:
+    for ref, n in ((right, count), (left, count)):
         @pl.loop(0, n)
         def _(v, ref=ref, slot=slot):
             at = pl.multiple_of((v + slot) * SUB, SUB)
@@ -57,30 +53,47 @@
             near[row, base : base + 2 * SUB, :] = jnp.where(even, high, low).astype(BF16)
             far[row, base : base + 2 * SUB, :] = jnp.where(even, low, high).astype(BF16)
 
-    lane = lane_index((rows, cols))
+
+def sides_kernel(right, left, bonds, side, own, flat):
+    count, rows, cols = right.shape
+    group = LANES // TAPS
+    pitch = rows + 1
+    signs = len(ODD) * TAPS
+
     for which, ref in enumerate((right, left)):
-        for block in range(count // group):
-            total = jnp.zeros((rows, cols), F32)
-            for t in range(group):
-                moved = pltpu.roll(ref[block * group + t].astype(F32), RANGE + TAPS * t, 1)
-                total = jnp.where(lane // TAPS == t, moved, total)
-            side[which * (count // group) + block] = total.astype(BF16)
-    total = jnp.zeros((rows, cols), F32)
-    for t in range(len(ODD) * TAPS):
-        moved = pltpu.roll(sign_of(ODD[t // TAPS], t % TAPS), RANGE + TAPS * t, 1)
-        total = jnp.where(lane // TAPS == t, moved, total)
-    side[2 * (count // group)] = total.astype(BF16)
-
-
-def main_kernel(widths, parity, hop, right, left, bonds, near, far, side, out,
-                value, rim, coef, band, mats, acc, back_a, first_a, back_b, first_b):
+        @pl.loop(0, count, unroll=4)
+        def _(v, which=which, ref=ref):
+            flat[pl.ds((v + which * count) * pitch, rows), :] = ref[v].astype(F32)
+
+    for t in range(signs):
+        at = (2 * count + t) * pitch
+        flat[at : at + rows, :] = (2 * bonds[ODD[t // TAPS], t % TAPS] - 1).astype(F32)
+
+    lane = lane_index((2 * SUB, cols)) // TAPS
+
+    @pl.loop(0, (2 * count + signs) // (2 * SUB))
+    def _(pair):
+        at = pl.multiple_of(pair * 2 * SUB, 2 * SUB)
+        for tile in range(rows // group):
+            total = jnp.zeros((2 * SUB, cols), F32)
+            for r in range(group):
+                row = tile * group + r
+                strip = jnp.concatenate(
+                    [flat[pl.ds((at + half * SUB) * pitch + row, SUB, stride=pitch), :] for half in range(2)], axis=0
+                )
+                total = jnp.where(lane == r, pltpu.roll(strip, (RANGE + TAPS * r) % LANES, 1), total)
+            side[tile, pl.ds(at, 2 * SUB), :] = total.astype(BF16)
+
+    own[...] = side[:, 2 * count :, :]
+
+
+def main_kernel(widths, parity, hop, right, left, bonds, near, far, side, own, out,
+                value, coef, band, mats, matsl, acc, back_a, first_a, back_b, first_b):
     count, rows, cols = right.shape
     even = parity[0] == 0
     group = LANES // TAPS
-    blocks = count // group
     stride = rows + 2 * SUB + 1
     period = 2 * TAPS
-    lane_all = lane_index((rows, cols))
 
     def scale_of(a, index):
         return hop[a, index % RANGE] * (1.0 if index < RANGE else -1.0)
@@ -101,50 +114,36 @@
             source = low if index < RANGE else high
             coef[a * TAPS + index, where : where + 1, :] = source[slot : slot + 1] * scale_of(a, index)
 
-    inner_lane = lane_all % TAPS
-    last = inner_lane < RANGE
-    signs = side[2 * blocks].astype(F32)
-    weights = {}
-    for which in range(2):
-        for a in ODD:
-            for k in range(1, RANGE + 1):
-                if which == 0:
-                    tops = pltpu.roll(coef[a * TAPS + k - 1, SUB : SUB + rows, :], RANGE, 1)
-                    bottoms = pltpu.roll(coef[a * TAPS + RANGE + k - 1, SUB : SUB + rows, :], RANGE, 1)
-                else:
-                    slot = ODD.index(a) * TAPS + k - 1
-                    bottoms = pltpu.roll(signs, (k - TAPS * slot) % LANES, 1) * scale_of(a, k - 1)
-                    tops = pltpu.roll(signs, (-k - TAPS * (slot + RANGE)) % LANES, 1) * scale_of(a, RANGE + k - 1)
-                one = jnp.where(lane_all < RANGE, tops, bottoms)
-                valid = ((lane_all < RANGE) & (lane_all + k >= RANGE)) | ((lane_all >= RANGE) & (lane_all - k < RANGE) & (lane_all < TAPS))
-                one = jnp.where(valid, one, 0.0)
-                for shift in (TAPS, 2 * TAPS, 4 * TAPS, 8 * TAPS):
-                    one = one + pltpu.roll(one, shift, 1)
-                weights[which, a, k] = one
-        for block in range(blocks):
-            packed = side[which * blocks + block].astype(F32)
+    tile_shape = (count, cols)
+    spot = lane_index((1, cols)) % TAPS
+    spots = lane_index(tile_shape) % TAPS
+    for tile in range(rows // group):
+        mine = own[tile].astype(F32)
+        theirs = side[tile, 2 * count :, :].astype(F32)
+        for which in range(2):
+            packed = side[tile, which * count : (which + 1) * count, :].astype(F32)
             total = {}
             for k in range(1, RANGE + 1):
-                moved = jnp.where(last, pltpu.roll(packed, LANES - k, 1), pltpu.roll(packed, k, 1))
+                moved = jnp.where(spots < RANGE, pltpu.roll(packed, LANES - k, 1), pltpu.roll(packed, k, 1))
                 for a in ODD:
-                    term = weights[which, a, k] * moved
+                    slot = ODD.index(a) * TAPS + k - 1
+                    if which == 0:
+                        tops, bottoms = mine[slot : slot + 1], mine[slot + RANGE : slot + RANGE + 1]
+                        weight = jnp.where(spot < RANGE, tops * scale_of(a, k - 1), bottoms * scale_of(a, RANGE + k - 1))
+                    else:
+                        tops = pltpu.roll(theirs, LANES - k, 1)[slot + RANGE : slot + RANGE + 1]
+                        bottoms = pltpu.roll(theirs, k, 1)[slot : slot + 1]
+                        weight = jnp.where(spot < RANGE, tops * scale_of(a, RANGE + k - 1), bottoms * scale_of(a, k - 1))
+                    valid = ((spot < RANGE) & (spot + k >= RANGE)) | ((spot >= RANGE) & (spot - k < RANGE))
+                    term = jnp.where(valid, weight, 0.0) * moved
                     total[a] = term if k == 1 else total[a] + term
             for a in ODD:
-                band[which * blocks + block, ODD.index(a)] = total[a]
-
-        ref = (right, left)[which]
-
-        @pl.loop(0, blocks)
-        def _(block, which=which, ref=ref):
-            for o in range(len(ODD)):
-                packed = band[which * blocks + block, o]
-                for t in range(group):
-                    moved = pltpu.roll(packed, (LANES - RANGE - TAPS * t) % LANES, 1)
-                    moved = jnp.where((lane_all < RANGE) | (lane_all >= cols - RANGE), moved, 0.0)
-                    rim[which, o, pl.ds((block * group + t) * (rows + 1), rows), :] = moved
-            for t in range(group):
-                v = block * group + t
-                value[which, pl.ds(v * stride + SUB, rows), :] = ref[v].astype(F32)
+                band[which, ODD.index(a), tile] = total[a]
+
+    for which, ref in enumerate((right, left)):
+        @pl.loop(0, count, unroll=4)
+        def _(v, which=which, ref=ref):
+            value[which, pl.ds(v * stride + SUB, rows), :] = ref[v].astype(F32)
 
         for base in range(0, count, 2 * SUB):
             for row in range(RANGE):
@@ -172,26 +171,27 @@
             low = (total - high.astype(F32)).astype(BF16)
             o = ODD.index(a)
             for part, piece in enumerate((high, low)):
-                mats[slot, part * cols : (part + 1) * cols, o * cols : (o + 1) * cols] = (
-                    jnp.concatenate([piece] * (cols // period), axis=0) * within
-                )
+                block = jnp.concatenate([piece] * (cols // period), axis=0) * within
+                mats[slot, part * cols : (part + 1) * cols, o * cols : (o + 1) * cols] = block
+                matsl[slot, o * cols : (o + 1) * cols, part * cols : (part + 1) * cols] = block
+
+    rim_lane = (lane_index(tile_shape) < RANGE) | (lane_index(tile_shape) >= cols - RANGE)
 
     def stencil(row, part, slot, back, first):
         matrices(row, slot)
         here_lanes = slice(part * cols, (part + 1) * cols)
+        tile = row // group
+        turn = (2 * LANES - RANGE - TAPS * (row % group)) % LANES
         for which, target in ((0, first), (1, back)):
             middle = jnp.concatenate(
                 [value[which, pl.ds(g * SUB * stride + row + SUB, SUB, stride=stride), :] for g in range(count // SUB)], axis=0
             ).astype(BF16)
+            middle = jnp.concatenate([middle, middle], axis=1)
+            dims = (((1,), (which,)), ((), ()))
+            both = lax.dot_general(middle, (mats, matsl)[which][slot], dims, preferred_element_type=F32)
             for o, a in enumerate(ODD):
-                mine = slice(o * cols, (o + 1) * cols)
-                dims = (((1,), (which,)), ((), ()))
-                total = lax.dot_general(middle, mats[slot, :cols, mine], dims, preferred_element_type=F32)
-                total = total + lax.dot_general(middle, mats[slot, cols:, mine], dims, preferred_element_type=F32)
-                beyond = jnp.concatenate(
-                    [rim[which, o, pl.ds(g * SUB * (rows + 1) + row, SUB, stride=rows + 1), :] for g in range(count // SUB)], axis=0
-                )
-                target[a * count : (a + 1) * count, here_lanes] = (total + beyond).astype(BF16)
+                beyond = jnp.where(rim_lane, pltpu.roll(band[which, o, tile], turn, 1), 0.0)
+                target[a * count : (a + 1) * count, here_lanes] = (both[:, o * cols : (o + 1) * cols] + beyond).astype(BF16)
             factors = {}
             for a in EVEN:
                 for index in range(TAPS):
@@ -269,25 +269,35 @@
 def on_device(left, right, bond_signs, hop):
     count, rows, cols = right.shape
     wide, narrow = lax.axis_size("wide"), lax.axis_size("narrow")
-    group = LANES // TAPS
-    blocks = 2 * (count // group) + 1
     edge_rows = 2 * count + len(EVEN) * TAPS
+    side_rows = 2 * count + len(ODD) * TAPS
+    tiles = rows * TAPS // LANES
     parity = (lax.axis_index("wide") % 2).astype(jnp.int32).reshape(1)
     smem = pl.BlockSpec(memory_space=pltpu.SMEM)
     vmem = pl.BlockSpec(memory_space=pltpu.VMEM)
-
-    near, far, side = pl.pallas_call(
-        pack_kernel,
+    params = pltpu.CompilerParams(vmem_limit_bytes=VMEM_LIMIT)
+
+    near, far = pl.pallas_call(
+        rows_kernel,
+        out_shape=(jax.ShapeDtypeStruct((RANGE, edge_rows, cols), BF16),) * 2,
+        in_specs=[smem, vmem, vmem, vmem],
+        out_specs=(vmem, vmem),
+        scratch_shapes=[VMEM((edge_rows * SUB, cols), F32), VMEM((edge_rows * SUB, cols), F32)],
+        compiler_params=params,
+        name="edge_rows",
+    )(parity, right, left, bond_signs)
+    side, own = pl.pallas_call(
+        sides_kernel,
         out_shape=(
-            jax.ShapeDtypeStruct((RANGE, edge_rows, cols), BF16),
-            jax.ShapeDtypeStruct((RANGE, edge_rows, cols), BF16),
-            jax.ShapeDtypeStruct((blocks, rows, cols), BF16),
+            jax.ShapeDtypeStruct((tiles, side_rows, cols), BF16),
+            jax.ShapeDtypeStruct((tiles, side_rows - 2 * count, cols), BF16),
         ),
-        in_specs=[smem, vmem, vmem, vmem],
-        out_specs=(vmem, vmem, vmem),
-        scratch_shapes=[VMEM((edge_rows * SUB, cols), F32), VMEM((edge_rows * SUB, cols), F32)],
-        name="pack",
-    )(parity, right, left, bond_signs)
+        in_specs=[vmem, vmem, vmem],
+        out_specs=(vmem, vmem),
+        scratch_shapes=[VMEM((side_rows * (rows + 1) + SUB, cols), F32)],
+        compiler_params=params,
+        name="edge_columns",
+    )(right, left, bond_signs)
 
     far = swap(far, "wide", [(i, (i + 1) % wide if i % 2 else (i - 1) % wide) for i in range(wide)])
     near = swap(near, "wide", [(i, i ^ 1) for i in range(wide)])
@@ -305,18 +315,19 @@
     partial = pl.pallas_call(
         lambda *refs: main_kernel((wide, narrow), *refs),
         out_shape=jax.ShapeDtypeStruct(blocked if direct else (size, size), BF16),
-        in_specs=[smem, smem] + [vmem] * 6,
+        in_specs=[smem, smem] + [vmem] * 7,
         out_specs=vmem,
         scratch_shapes=[
             VMEM((2, count * (rows + 2 * SUB + 1) + SUB, cols), F32),
-            VMEM((2, len(ODD), count * (rows + 1) + SUB, cols), F32),
             VMEM((OPS * TAPS, rows + 2 * SUB, cols), F32),
-            VMEM((blocks - 1, len(ODD), rows, cols), F32),
+            VMEM((2, len(ODD), tiles, count, cols), F32),
             VMEM((4, 2 * cols, len(ODD) * cols), BF16),
+            VMEM((4, len(ODD) * cols, 2 * cols), BF16),
             VMEM((size, size), F32),
         ] + [VMEM((size, 2 * cols), BF16)] * 4,
+        compiler_params=params,
         name="moments",
-    )(parity, hop, right, left, bond_signs, near, far, side)
+    )(parity, hop, right, left, bond_signs, near, far, side, own)
     if not direct:
         partial = partial.reshape(wide, OPS * per_left, narrow, OPS * per_right).transpose(0, 2, 1, 3).reshape(blocked)
     got = lax.all_to_all(partial, ("wide", "narrow"), 0, 0, tiled=True)

time: 52.9 us -> 45.9 us (0.87)
  Pallas kernels: 27.8 us -> 18 us
  local copies, waits for them, and re-layouts: 0.67 us -> 3.69 us
  waiting for transfers between devices: 3.86 us -> 2.82 us
    pallas_call x1, Pallas kernels: 22 us -> 13.8 us  [on_device(): pl.pallas_call(lambda *refs: main_kernel((wide, narrow), *refs), out_shap...]
    unnamed x6 -> x14, local copies, waits for them, and re-layouts: 0.67 us -> 3.69 us
    pallas_call x1 -> x2, Pallas kernels: 4.18 us -> 2.6 us  [the longest x1 1.67 us: on_device(): pl.pallas_call(sides_kernel, out_shape=(jax.ShapeDtypeStruct((tiles, side...]
    ppermute x3, waiting for transfers between devices: 3.86 us -> 2.82 us  [swap(): return lax.ppermute(array, axis, pairs)]
    all_to_all x1, blocking collectives: 12.8 us -> 13.3 us  [on_device(): got = lax.all_to_all(partial, ('wide', 'narrow'), 0, 0, tiled=True)]
  transfers between devices with their start and end apart: 3 -> 3, of which waited for: 2 -> 1; matrix products, arithmetic and copies ran while one was open for 0% -> 0% of each run, Pallas kernels for 0% -> 2%
where the time goes in v2:
time: 45.9 us; the launch traced here: 45.7 us
  Pallas kernels  18 us (39%)
  blocking collectives  13.3 us (29%)
  starting transfers between devices  7.76 us (17%)
  local copies, waits for them, and re-layouts  3.69 us (8%)
  waiting for transfers between devices  2.82 us (6%)
    pallas_call x1, Pallas kernels, on_device(): pl.pallas_call(lambda *refs: main_kernel((wide, narrow), *refs), out_shap...  13.8 us
    all_to_all x1, blocking collectives, on_device(): got = lax.all_to_all(partial, ('wide', 'narrow'), 0, 0, tiled=True)  13.3 us
    ppermute x3, starting transfers between devices, swap(): return lax.ppermute(array, axis, pairs)  7.76 us
    unnamed x14, local copies, waits for them, and re-layouts  3.69 us
    ppermute x3, waiting for transfers between devices, swap(): return lax.ppermute(array, axis, pairs)  2.82 us
    pallas_call x1, Pallas kernels, on_device(): pl.pallas_call(sides_kernel, out_shape=(jax.ShapeDtypeStruct((tiles, side...  1.67 us
    pallas_call x1, Pallas kernels, on_device(): pl.pallas_call(lambda *refs: sum_kernel(factor, *refs), out_shape=jax.Sha...  1.63 us
    pallas_call x1, Pallas kernels, on_device(): pl.pallas_call(rows_kernel, out_shape=(jax.ShapeDtypeStruct((RANGE, edge_...  0.94 us
  transfers between devices with their start and end apart: 3, of which 1 were waited for; matrix products, arithmetic and copies ran while one was open for 0% of the time, Pallas kernels for 2%

profile of v2, /device:TPU:0, one launch (start us, length us, event | category | flops | bytes accessed | tf_op | source)
XLA Modules:
  0.0 45.7 jit_solution(13382469111688835294)
XLA Ops:
  0.0 0.0 copy-start
  0.0 1.2 %copy-done = bf16[64,64,128]{2,1,0:T(8,128)(2,1)S(1)} copy-done((bf16[64,64,128]{2,1,0:T(8,128)(2,1)S(1)}, bf16[64,64,128]{2,1,0:T(8,128)(2,1)}, u32[]{:S(2)}) %copy-start) | copy-done | bytes 1048600
  1.2 0.0 copy-start.2
  1.2 1.2 %copy-done.2 = bf16[64,64,128]{2,1,0:T(8,128)(2,1)S(1)} copy-done((bf16[64,64,128]{2,1,0:T(8,128)(2,1)S(1)}, bf16[64,64,128]{2,1,0:T(8,128)(2,1)}, u32[]{:S(2)}) %copy-start.2) | copy-done | bytes 1048600
  2.5 0.0 copy-start.4
  2.5 1.2 %copy-done.4 = s32[4,8,64,128]{3,2,1,0:T(8,128)S(1)} copy-done((s32[4,8,64,128]{3,2,1,0:T(8,128)S(1)}, s32[4,8,64,128]{3,2,1,0:T(8,128)}, u32[]{:S(2)}) %copy-start.4) | copy-done | bytes 1048600
  3.7 0.0 copy-start.1
  3.7 0.0 copy-start.3
  3.7 0.0 copy-start.5
  3.7 1.7 %edge_columns.1 = (bf16[4,144,128]{2,1,0:T(8,128)(2,1)S(1)}, bf16[4,16,128]{2,1,0:T(8,128)(2,1)S(1)}) custom-call(bf16[64,64,128]{2,1,0:T(8,128)(2,1)S(1)} %copy-done, bf16[64,64,128]{2,1,0:T(8,128)(2,1)S(1)} %copy-done.2, s32[4,8,64,128]{3,2,1,0:T(8,128)S(1)} %copy-done.4), custom_call_target="tpu_custom_call" | custom-call | tf_op jit(solution)/shard_map/edge_columns/pallas_call | solution.py:289
  5.4 3.0 %collective-permute-start.2 = (bf16[4,144,128]{2,1,0:T(8,128)(2,1)S(1)}, bf16[4,144,128]{2,1,0:T(8,128)(2,1)S(1)}, u32[]{:S(2)}, u32[]{:S(2)}) collective-permute-start(bf16[4,144,128]{2,1,0:T(8,128)(2,1)S(1)} %get-tuple-element.11), channel_id=1, source_target_pairs={{0,1},{1,0},{2,3},{3,2},{4,5},{5,4},{6,7},{7,6},{8,9},{9,8},{10,11... | collective-permute-start | bytes 442376 | tf_op jit(solution)/shard_map/ppermute | solution.py:266
  8.4 0.0 copy-done.1
  8.4 0.0 copy-done.3
  8.4 0.0 copy-done.5
  8.4 0.9 %edge_rows.1 = (bf16[4,144,128]{2,1,0:T(8,128)(2,1)S(1)}, bf16[4,144,128]{2,1,0:T(8,128)(2,1)S(1)}) custom-call(s32[1]{0:T(128)} %bitcast.parity.refs_0_, bf16[64,64,128]{2,1,0:T(8,128)(2,1)S(1)} %copy-done.1, bf16[64,64,128]{2,1,0:T(8,128)(2,1)S(1)} %copy-done.3, s32[4,8,64,128]{3,2,1,0:T(8,128)S(1)} %copy-done.5), custom_call_target="tpu_custom_call" | custom-call | tf_op jit(solution)/shard_map/edge_rows/pallas_call | solution.py:280
  9.3 0.0 copy-start.6
  9.3 0.1 collective-permute-start
  9.4 4.7 %collective-permute-start.1 = (bf16[4,144,128]{2,1,0:T(8,128)(2,1)S(1)}, bf16[4,144,128]{2,1,0:T(8,128)(2,1)S(1)}, u32[]{:S(2)}, u32[]{:S(2)}) collective-permute-start(bf16[4,144,128]{2,1,0:T(8,128)(2,1)S(1)} %get-tuple-element.10), channel_id=1, source_target_pairs={{0,30},{2,4},{4,2},{6,8},{8,6},{10,12},{12,10},{14,16},{16,14},{18... | collective-permute-start | bytes 442376 | tf_op jit(solution)/shard_map/ppermute | solution.py:266
  14.1 0.0 collective-permute-done.2.refs_7_
  14.1 0.0 collective-permute-done.refs_5_
  14.1 2.8 %collective-permute-done.1.refs_6_ = bf16[4,144,128]{2,1,0:T(8,128)(2,1)S(1)} collective-permute-done((bf16[4,144,128]{2,1,0:T(8,128)(2,1)S(1)}, bf16[4,144,128]{2,1,0:T(8,128)(2,1)S(1)}, u32[]{:S(2)}, u32[]{:S(2)}) %collective-permute-start.1) | collective-permute-done | bytes 147488 | tf_op jit(solution)/shard_map/ppermute | solution.py:266
  16.9 0.0 copy-done.6
  16.9 13.8 %moments.1 = bf16[32,16,128]{2,1,0:T(8,128)(2,1)S(1)} custom-call(s32[1]{0:T(128)} %bitcast.parity.refs_0_, f32[4,4]{1,0:T(4,128)S(1)} %copy-done.6, bf16[64,64,128]{2,1,0:T(8,128)(2,1)S(1)} %copy-done.1, bf16[64,64,128]{2,1,0:T(8,128)(2,1)S(1)} %copy-done.3, s32[4,8,64,128]{3,2,1,0:T(8,128)S(1)} %copy-done.5, ...), custom_call_target="tpu_custom_call" | custom-call | tf_op jit(solution)/shard_map/moments/pallas_call | solution.py:315
  30.7 13.3 %all_to_all.5.refs_0_ = bf16[32,16,128]{2,1,0:T(8,128)(2,1)} all-to-all(bf16[32,16,128]{2,1,0:T(8,128)(2,1)S(1)} %moments.1), channel_id=1, replica_groups=mesh['wide'=16,'narrow'=2] {'wide','narrow'}, dimensions={0} | all-to-all | bytes 262144 | tf_op jit(solution)/shard_map/all_to_all | solution.py:333
  44.1 1.6 %total.1 = f32[16,4,32]{2,1,0:T(4,128)} custom-call(bf16[32,16,128]{2,1,0:T(8,128)(2,1)} %all_to_all.5.refs_0_), custom_call_target="tpu_custom_call" | custom-call | tf_op jit(solution)/shard_map/total/pallas_call | solution.py:335
Async XLA Ops:
  0.0 1.2 %copy-start = (bf16[64,64,128]{2,1,0:T(8,128)(2,1)S(1)}, bf16[64,64,128]{2,1,0:T(8,128)(2,1)}, u32[]{:S(2)}) copy-start(bf16[64,64,128]{2,1,0:T(8,128)(2,1)} %refs_2_.1) | copy-start | bytes 3145732
  1.2 1.2 %copy-start.2 = (bf16[64,64,128]{2,1,0:T(8,128)(2,1)S(1)}, bf16[64,64,128]{2,1,0:T(8,128)(2,1)}, u32[]{:S(2)}) copy-start(bf16[64,64,128]{2,1,0:T(8,128)(2,1)} %refs_3_.1) | copy-start | bytes 3145732
  2.5 1.2 %copy-start.4 = (s32[4,8,64,128]{3,2,1,0:T(8,128)S(1)}, s32[4,8,64,128]{3,2,1,0:T(8,128)}, u32[]{:S(2)}) copy-start(s32[4,8,64,128]{3,2,1,0:T(8,128)} %refs_4_.1) | copy-start | bytes 3145732
  3.7 4.7 %copy-start.1 = (bf16[64,64,128]{2,1,0:T(8,128)(2,1)S(1)}, bf16[64,64,128]{2,1,0:T(8,128)(2,1)}, u32[]{:S(2)}) copy-start(bf16[64,64,128]{2,1,0:T(8,128)(2,1)} %refs_2_.1) | copy-start | bytes 3145732
  3.7 4.7 %copy-start.3 = (bf16[64,64,128]{2,1,0:T(8,128)(2,1)S(1)}, bf16[64,64,128]{2,1,0:T(8,128)(2,1)}, u32[]{:S(2)}) copy-start(bf16[64,64,128]{2,1,0:T(8,128)(2,1)} %refs_3_.1) | copy-start | bytes 3145732
  3.7 4.7 %copy-start.5 = (s32[4,8,64,128]{3,2,1,0:T(8,128)S(1)}, s32[4,8,64,128]{3,2,1,0:T(8,128)}, u32[]{:S(2)}) copy-start(s32[4,8,64,128]{3,2,1,0:T(8,128)} %refs_4_.1) | copy-start | bytes 3145732
  5.4 8.7 %collective-permute-start.2 = (bf16[4,144,128]{2,1,0:T(8,128)(2,1)S(1)}, bf16[4,144,128]{2,1,0:T(8,128)(2,1)S(1)}, u32[]{:S(2)}, u32[]{:S(2)}) collective-permute-start(bf16[4,144,128]{2,1,0:T(8,128)(2,1)S(1)} %get-tuple-element.11), channel_id=1, source_target_pairs={{0,1},{1,0},{2,3},{3,2},{4,5},{5,4},{6,7},{7,6},{8,9},{9,8},{10,11... | collective-permute-start | bytes 442376 | tf_op jit(solution)/shard_map/ppermute | solution.py:266
  9.3 7.6 %copy-start.6 = (f32[4,4]{1,0:T(4,128)S(1)}, f32[4,4]{1,0:T(4,128)}, u32[]{:S(2)}) copy-start(f32[4,4]{1,0:T(4,128)} %refs_1_.1) | copy-start | bytes 196
  9.3 4.7 %collective-permute-start = (bf16[4,144,128]{2,1,0:T(8,128)(2,1)S(1)}, bf16[4,144,128]{2,1,0:T(8,128)(2,1)S(1)}, u32[]{:S(2)}, u32[]{:S(2)}) collective-permute-start(bf16[4,144,128]{2,1,0:T(8,128)(2,1)S(1)} %get-tuple-element.9), channel_id=1, source_target_pairs={{0,2},{2,0},{4,6},{6,4},{8,10},{10,8},{12,14},{14,12},{16,18},{18,... | collective-permute-start | bytes 442376 | tf_op jit(solution)/shard_map/ppermute | solution.py:266
  9.4 7.5 %collective-permute-start.1 = (bf16[4,144,128]{2,1,0:T(8,128)(2,1)S(1)}, bf16[4,144,128]{2,1,0:T(8,128)(2,1)S(1)}, u32[]{:S(2)}, u32[]{:S(2)}) collective-permute-start(bf16[4,144,128]{2,1,0:T(8,128)(2,1)S(1)} %get-tuple-element.10), channel_id=1, source_target_pairs={{0,30},{2,4},{4,2},{6,8},{8,6},{10,12},{12,10},{14,16},{16,14},{18... | collective-permute-start | bytes 442376 | tf_op jit(solution)/shard_map/ppermute | solution.py:266

commit v3 on v2

--- a/solution.py
+++ b/solution.py
@@ -6,6 +6,7 @@
 from jax.experimental import pallas as pl
 from jax.experimental.pallas import tpu as pltpu
 from jax.sharding import PartitionSpec as P
+
 
 OPS = 4
 RANGE = 4
@@ -24,23 +25,36 @@
     return lax.broadcasted_iota(jnp.int32, shape, len(shape) - 1)
 
 
-def rows_kernel(parity, right, left, bonds, near, far, head, tail):
-    count, rows, cols = right.shape
+def rows_kernel(parity, right, left, bonds, near, far, head, tail, ends, signs, sems):
+    count, rows, _ = right.shape
     even = parity[0] == 0
 
+    copies = []
+    for end, at in enumerate((0, rows - 2 * SUB)):
+        for which, ref in enumerate((right, left)):
+            copies.append((ref.at[:, pl.ds(at, 2 * SUB), :], ends.at[end, which]))
+    for end, at in enumerate((0, rows - SUB)):
+        for o, a in enumerate(EVEN):
+            copies.append((bonds.at[a, :, pl.ds(at, SUB), :], signs.at[end, o]))
+    copies = [pltpu.make_async_copy(src, dst, sems.at[n]) for n, (src, dst) in enumerate(copies)]
+    for copy in copies:
+        copy.start()
+    for copy in copies:
+        copy.wait()
+
     slot = 0
-    for ref, n in ((right, count), (left, count)):
-        @pl.loop(0, n)
-        def _(v, ref=ref, slot=slot):
+    for which in range(2):
+        @pl.loop(0, count, unroll=4)
+        def _(v, which=which, slot=slot):
             at = pl.multiple_of((v + slot) * SUB, SUB)
-            head[pl.ds(at, SUB), :] = ref[v, : 2 * SUB, :].astype(F32)[:SUB]
-            tail[pl.ds(at, SUB), :] = ref[v, rows - 2 * SUB :, :].astype(F32)[SUB:]
-
-        slot += n
-    for a in EVEN:
+            head[pl.ds(at, SUB), :] = ends[0, which, v].astype(F32)[:SUB]
+            tail[pl.ds(at, SUB), :] = ends[1, which, v].astype(F32)[SUB:]
+
+        slot += count
+    for o in range(len(EVEN)):
         for index in range(TAPS):
-            head[slot * SUB : slot * SUB + SUB, :] = (2 * bonds[a, index, :SUB, :] - 1).astype(F32)
-            tail[slot * SUB : slot * SUB + SUB, :] = (2 * bonds[a, index, rows - SUB :, :] - 1).astype(F32)
+            head[slot * SUB : slot * SUB + SUB, :] = (2 * signs[0, o, index] - 1).astype(F32)
+            tail[slot * SUB : slot * SUB + SUB, :] = (2 * signs[1, o, index] - 1).astype(F32)
             slot += 1
     for base in range(0, slot, 2 * SUB):
         for row in range(RANGE):
@@ -88,7 +102,7 @@
 
 
 def main_kernel(widths, parity, hop, right, left, bonds, near, far, side, own, out,
-                value, coef, band, mats, matsl, acc, back_a, first_a, back_b, first_b):
+                value, coef, band, acc):
     count, rows, cols = right.shape
     even = parity[0] == 0
     group = LANES // TAPS
@@ -161,7 +175,8 @@
     near_diagonal = lane_index((cols, cols)) - lax.broadcasted_iota(jnp.int32, (cols, cols), 0)
     within = jnp.where((near_diagonal >= -TAPS) & (near_diagonal < TAPS), 1.0, 0.0).astype(BF16)
 
-    def matrices(row, slot):
+    def matrices(row):
+        pieces = {}
         for a in ODD:
             total = jnp.zeros(tile, F32)
             for k in range(1, RANGE + 1):
@@ -169,29 +184,30 @@
                 total = jnp.where(gap == k, coef[a * TAPS + RANGE + k - 1, pl.ds(row + SUB, period, stride=0), :], total)
             high = total.astype(BF16)
             low = (total - high.astype(F32)).astype(BF16)
-            o = ODD.index(a)
             for part, piece in enumerate((high, low)):
-                block = jnp.concatenate([piece] * (cols // period), axis=0) * within
-                mats[slot, part * cols : (part + 1) * cols, o * cols : (o + 1) * cols] = block
-                matsl[slot, o * cols : (o + 1) * cols, part * cols : (part + 1) * cols] = block
+                pieces[part, a] = jnp.concatenate([piece] * (cols // period), axis=0) * within
+        right_side = jnp.concatenate([jnp.concatenate([pieces[part, a] for a in ODD], axis=1) for part in range(2)], axis=0)
+        left_side = jnp.concatenate([jnp.concatenate([pieces[part, a] for part in range(2)], axis=1) for a in ODD], axis=0)
+        return right_side, left_side
 
     rim_lane = (lane_index(tile_shape) < RANGE) | (lane_index(tile_shape) >= cols - RANGE)
 
-    def stencil(row, part, slot, back, first):
-        matrices(row, slot)
-        here_lanes = slice(part * cols, (part + 1) * cols)
+    def stencil(row):
+        bands = matrices(row)
+        results = []
         tile = row // group
         turn = (2 * LANES - RANGE - TAPS * (row % group)) % LANES
-        for which, target in ((0, first), (1, back)):
+        for which in range(2):
+            done = {}
             middle = jnp.concatenate(
                 [value[which, pl.ds(g * SUB * stride + row + SUB, SUB, stride=stride), :] for g in range(count // SUB)], axis=0
             ).astype(BF16)
             middle = jnp.concatenate([middle, middle], axis=1)
             dims = (((1,), (which,)), ((), ()))
-            both = lax.dot_general(middle, (mats, matsl)[which][slot], dims, preferred_element_type=F32)
+            both = lax.dot_general(middle, bands[which], dims, preferred_element_type=F32)
             for o, a in enumerate(ODD):
                 beyond = jnp.where(rim_lane, pltpu.roll(band[which, o, tile], turn, 1), 0.0)
-                target[a * count : (a + 1) * count, here_lanes] = (both[:, o * cols : (o + 1) * cols] + beyond).astype(BF16)
+                done[a] = [(both[:, o * cols : (o + 1) * cols] + beyond).astype(BF16)]
             factors = {}
             for a in EVEN:
                 for index in range(TAPS):
@@ -213,38 +229,30 @@
                     for a in EVEN:
                         sums[a].append(total[a])
                 for a in EVEN:
-                    at = a * count + pair * 2 * SUB
-                    target[at : at + 2 * SUB, here_lanes] = jnp.concatenate(sums[a], axis=0).astype(BF16)
-
-    def product(back, first):
-        acc[...] += lax.dot_general(back[...], first[...], (((1,), (1,)), ((), ())), preferred_element_type=F32)
-
-    back_b[...] = jnp.zeros_like(back_b)
-    first_b[...] = jnp.zeros_like(first_b)
-
-    @pl.loop(0, rows // 4)
+                    done.setdefault(a, []).append(jnp.concatenate(sums[a], axis=0).astype(BF16))
+            results.append(jnp.concatenate([piece for a in range(OPS) for piece in done[a]], axis=0))
+        return results
+
+    @pl.loop(0, rows // 16)
     def _(step):
-        product(back_b, first_b)
-        for part in range(2):
-            stencil(step * 4 + part, part, part, back_a, first_a)
-        product(back_a, first_a)
-        for part in range(2):
-            stencil(step * 4 + 2 + part, part, 2 + part, back_b, first_b)
-
-    product(back_b, first_b)
+        for start in range(0, 16, 2):
+            found = [stencil(step * 16 + start + n) for n in range(2)]
+            first = jnp.concatenate([one[0] for one in found], axis=1)
+            back = jnp.concatenate([one[1] for one in found], axis=1)
+            acc[...] += lax.dot_general(back, first, (((1,), (1,)), ((), ())), preferred_element_type=F32)
 
     parts_left, parts_right = widths
     per_left, per_right = count // parts_left, count // parts_right
     size = OPS * count
 
-    def order(parts, per, dim):
+    def order(per, dim):
         new = lax.broadcasted_iota(jnp.int32, (size, size), dim)
         old = lax.broadcasted_iota(jnp.int32, (size, size), 1 - dim)
         part, rest = new // (OPS * per), new % (OPS * per)
         return jnp.where(old == (rest // per) * count + part * per + rest % per, 1.0, 0.0).astype(BF16)
 
-    moved = jnp.dot(order(parts_left, per_left, 0), acc[...].astype(BF16), preferred_element_type=F32).astype(BF16)
-    moved = jnp.dot(moved, order(parts_right, per_right, 1), preferred_element_type=F32).astype(BF16)
+    moved = jnp.dot(order(per_left, 0), acc[...].astype(BF16), preferred_element_type=F32).astype(BF16)
+    moved = jnp.dot(moved, order(per_right, 1), preferred_element_type=F32).astype(BF16)
     if out.ndim == 2:
         out[...] = moved
     else:
@@ -277,12 +285,20 @@
     vmem = pl.BlockSpec(memory_space=pltpu.VMEM)
     params = pltpu.CompilerParams(vmem_limit_bytes=VMEM_LIMIT)
 
+    hbm = pl.BlockSpec(memory_space=pltpu.HBM)
+
     near, far = pl.pallas_call(
         rows_kernel,
         out_shape=(jax.ShapeDtypeStruct((RANGE, edge_rows, cols), BF16),) * 2,
-        in_specs=[smem, vmem, vmem, vmem],
+        in_specs=[smem, hbm, hbm, hbm],
         out_specs=(vmem, vmem),
-        scratch_shapes=[VMEM((edge_rows * SUB, cols), F32), VMEM((edge_rows * SUB, cols), F32)],
+        scratch_shapes=[
+            VMEM((edge_rows * SUB, cols), F32),
+            VMEM((edge_rows * SUB, cols), F32),
+            VMEM((2, 2, count, 2 * SUB, cols), BF16),
+            VMEM((2, len(EVEN), TAPS, SUB, cols), jnp.int32),
+            pltpu.SemaphoreType.DMA((4 + 2 * len(EVEN),)),
+        ],
         compiler_params=params,
         name="edge_rows",
     )(parity, right, left, bond_signs)
@@ -321,10 +337,8 @@
             VMEM((2, count * (rows + 2 * SUB + 1) + SUB, cols), F32),
             VMEM((OPS * TAPS, rows + 2 * SUB, cols), F32),
             VMEM((2, len(ODD), tiles, count, cols), F32),
-            VMEM((4, 2 * cols, len(ODD) * cols), BF16),
-            VMEM((4, len(ODD) * cols, 2 * cols), BF16),
             VMEM((size, size), F32),
-        ] + [VMEM((size, 2 * cols), BF16)] * 4,
+        ],
         compiler_params=params,
         name="moments",
     )(parity, hop, right, left, bond_signs, near, far, side, own)
@@ -349,6 +363,5 @@
         P(),
     )
     out_specs = P(None, "wide", "narrow")
-    return jax.shard_map(
-        on_device, mesh=mesh, in_specs=in_specs, out_specs=out_specs, check_vma=False
-    )
+
+    return jax.shard_map(on_device, mesh=mesh, in_specs=in_specs, out_specs=out_specs, check_vma=False)

time: 45.9 us -> 41.6 us (0.906)
  Pallas kernels: 18 us -> 13.7 us
    pallas_call x1, Pallas kernels: 13.8 us -> 9.81 us  [on_device(): pl.pallas_call(lambda *refs: main_kernel((wide, narrow), *refs), out_shap...]
  transfers between devices with their start and end apart: 3 -> 3, of which waited for: 1 -> 1; matrix products, arithmetic and copies ran while one was open for 0% -> 0% of each run, Pallas kernels for 2% -> 1%
where the time goes in v3:
time: 41.6 us; the launch traced here: 41.3 us
  Pallas kernels  13.7 us (33%)
  blocking collectives  13.3 us (32%)
  starting transfers between devices  7.76 us (19%)
  local copies, waits for them, and re-layouts  3.69 us (9%)
  waiting for transfers between devices  2.82 us (7%)
    all_to_all x1, blocking collectives, on_device(): got = lax.all_to_all(partial, ('wide', 'narrow'), 0, 0, tiled=True)  13.3 us
    pallas_call x1, Pallas kernels, on_device(): pl.pallas_call(lambda *refs: main_kernel((wide, narrow), *refs), out_shap...  9.81 us
    ppermute x3, starting transfers between devices, swap(): return lax.ppermute(array, axis, pairs)  7.76 us
    unnamed x14, local copies, waits for them, and re-layouts  3.69 us
    ppermute x3, waiting for transfers between devices, swap(): return lax.ppermute(array, axis, pairs)  2.82 us
    pallas_call x1, Pallas kernels, on_device(): pl.pallas_call(sides_kernel, out_shape=(jax.ShapeDtypeStruct((tiles, side...  1.67 us
    pallas_call x1, Pallas kernels, on_device(): pl.pallas_call(lambda *refs: sum_kernel(factor, *refs), out_shape=jax.Sha...  1.63 us
  transfers between devices with their start and end apart: 3, of which 1 were waited for; matrix products, arithmetic and copies ran while one was open for 0% of the time, Pallas kernels for 1%

profile of v3, /device:TPU:0, one launch (start us, length us, event | category | flops | bytes accessed | tf_op | source)
XLA Modules:
  0.0 41.3 jit_solution(5882852434950315502)
XLA Ops:
  0.0 0.0 copy-start
  0.0 1.2 %copy-done = bf16[64,64,128]{2,1,0:T(8,128)(2,1)S(1)} copy-done((bf16[64,64,128]{2,1,0:T(8,128)(2,1)S(1)}, bf16[64,64,128]{2,1,0:T(8,128)(2,1)}, u32[]{:S(2)}) %copy-start) | copy-done | bytes 1048600
  1.2 0.0 copy-start.2
  1.2 1.2 %copy-done.2 = bf16[64,64,128]{2,1,0:T(8,128)(2,1)S(1)} copy-done((bf16[64,64,128]{2,1,0:T(8,128)(2,1)S(1)}, bf16[64,64,128]{2,1,0:T(8,128)(2,1)}, u32[]{:S(2)}) %copy-start.2) | copy-done | bytes 1048600
  2.5 0.0 copy-start.4
  2.5 1.2 %copy-done.4 = s32[4,8,64,128]{3,2,1,0:T(8,128)S(1)} copy-done((s32[4,8,64,128]{3,2,1,0:T(8,128)S(1)}, s32[4,8,64,128]{3,2,1,0:T(8,128)}, u32[]{:S(2)}) %copy-start.4) | copy-done | bytes 1048600
  3.7 0.0 copy-start.1
  3.7 0.0 copy-start.3
  3.7 0.0 copy-start.5
  3.7 1.7 %edge_columns.1 = (bf16[4,144,128]{2,1,0:T(8,128)(2,1)S(1)}, bf16[4,16,128]{2,1,0:T(8,128)(2,1)S(1)}) custom-call(bf16[64,64,128]{2,1,0:T(8,128)(2,1)S(1)} %copy-done, bf16[64,64,128]{2,1,0:T(8,128)(2,1)S(1)} %copy-done.2, s32[4,8,64,128]{3,2,1,0:T(8,128)S(1)} %copy-done.4), custom_call_target="tpu_custom_call" | custom-call | tf_op jit(solution)/shard_map/edge_columns/pallas_call | solution.py:305
  5.4 3.0 %collective-permute-start.2 = (bf16[4,144,128]{2,1,0:T(8,128)(2,1)S(1)}, bf16[4,144,128]{2,1,0:T(8,128)(2,1)S(1)}, u32[]{:S(2)}, u32[]{:S(2)}) collective-permute-start(bf16[4,144,128]{2,1,0:T(8,128)(2,1)S(1)} %get-tuple-element.11), channel_id=1, source_target_pairs={{0,1},{1,0},{2,3},{3,2},{4,5},{5,4},{6,7},{7,6},{8,9},{9,8},{10,11... | collective-permute-start | bytes 442376 | tf_op jit(solution)/shard_map/ppermute | solution.py:274
  8.4 0.0 copy-done.1
  8.4 0.0 copy-done.3
  8.4 0.0 copy-done.5
  8.4 0.6 %edge_rows.1 = (bf16[4,144,128]{2,1,0:T(8,128)(2,1)S(1)}, bf16[4,144,128]{2,1,0:T(8,128)(2,1)S(1)}) custom-call(s32[1]{0:T(128)} %bitcast.parity.refs_0_, bf16[64,64,128]{2,1,0:T(8,128)(2,1)S(1)} %copy-done.1, bf16[64,64,128]{2,1,0:T(8,128)(2,1)S(1)} %copy-done.3, s32[4,8,64,128]{3,2,1,0:T(8,128)S(1)} %copy-done.5), custom_call_target="tpu_custom_call" | custom-call | tf_op jit(solution)/shard_map/edge_rows/pallas_call | solution.py:290
  9.0 0.0 copy-start.6
  9.0 0.1 collective-permute-start
  9.0 4.7 %collective-permute-start.1 = (bf16[4,144,128]{2,1,0:T(8,128)(2,1)S(1)}, bf16[4,144,128]{2,1,0:T(8,128)(2,1)S(1)}, u32[]{:S(2)}, u32[]{:S(2)}) collective-permute-start(bf16[4,144,128]{2,1,0:T(8,128)(2,1)S(1)} %get-tuple-element.10), channel_id=1, source_target_pairs={{0,30},{2,4},{4,2},{6,8},{8,6},{10,12},{12,10},{14,16},{16,14},{18... | collective-permute-start | bytes 442376 | tf_op jit(solution)/shard_map/ppermute | solution.py:274
  13.7 0.0 collective-permute-done.2.refs_7_
  13.7 0.0 collective-permute-done.refs_5_
  13.7 2.8 %collective-permute-done.1.refs_6_ = bf16[4,144,128]{2,1,0:T(8,128)(2,1)S(1)} collective-permute-done((bf16[4,144,128]{2,1,0:T(8,128)(2,1)S(1)}, bf16[4,144,128]{2,1,0:T(8,128)(2,1)S(1)}, u32[]{:S(2)}, u32[]{:S(2)}) %collective-permute-start.1) | collective-permute-done | bytes 147488 | tf_op jit(solution)/shard_map/ppermute | solution.py:274
  16.5 0.0 copy-done.6
  16.5 9.8 %moments.1 = bf16[32,16,128]{2,1,0:T(8,128)(2,1)S(1)} custom-call(s32[1]{0:T(128)} %bitcast.parity.refs_0_, f32[4,4]{1,0:T(4,128)S(1)} %copy-done.6, bf16[64,64,128]{2,1,0:T(8,128)(2,1)S(1)} %copy-done.1, bf16[64,64,128]{2,1,0:T(8,128)(2,1)S(1)} %copy-done.3, s32[4,8,64,128]{3,2,1,0:T(8,128)S(1)} %copy-done.5, ...), custom_call_target="tpu_custom_call" | custom-call | tf_op jit(solution)/shard_map/moments/pallas_call | solution.py:331
  26.3 13.3 %all_to_all.5.refs_0_ = bf16[32,16,128]{2,1,0:T(8,128)(2,1)} all-to-all(bf16[32,16,128]{2,1,0:T(8,128)(2,1)S(1)} %moments.1), channel_id=1, replica_groups=mesh['wide'=16,'narrow'=2] {'wide','narrow'}, dimensions={0} | all-to-all | bytes 262144 | tf_op jit(solution)/shard_map/all_to_all | solution.py:347
  39.7 1.6 %total.1 = f32[16,4,32]{2,1,0:T(4,128)} custom-call(bf16[32,16,128]{2,1,0:T(8,128)(2,1)} %all_to_all.5.refs_0_), custom_call_target="tpu_custom_call" | custom-call | tf_op jit(solution)/shard_map/total/pallas_call | solution.py:349
Async XLA Ops:
  0.0 1.2 %copy-start = (bf16[64,64,128]{2,1,0:T(8,128)(2,1)S(1)}, bf16[64,64,128]{2,1,0:T(8,128)(2,1)}, u32[]{:S(2)}) copy-start(bf16[64,64,128]{2,1,0:T(8,128)(2,1)} %refs_2_.1) | copy-start | bytes 3145732
  1.2 1.2 %copy-start.2 = (bf16[64,64,128]{2,1,0:T(8,128)(2,1)S(1)}, bf16[64,64,128]{2,1,0:T(8,128)(2,1)}, u32[]{:S(2)}) copy-start(bf16[64,64,128]{2,1,0:T(8,128)(2,1)} %refs_3_.1) | copy-start | bytes 3145732
  2.5 1.2 %copy-start.4 = (s32[4,8,64,128]{3,2,1,0:T(8,128)S(1)}, s32[4,8,64,128]{3,2,1,0:T(8,128)}, u32[]{:S(2)}) copy-start(s32[4,8,64,128]{3,2,1,0:T(8,128)} %refs_4_.1) | copy-start | bytes 3145732
  3.7 4.7 %copy-start.1 = (bf16[64,64,128]{2,1,0:T(8,128)(2,1)S(1)}, bf16[64,64,128]{2,1,0:T(8,128)(2,1)}, u32[]{:S(2)}) copy-start(bf16[64,64,128]{2,1,0:T(8,128)(2,1)} %refs_2_.1) | copy-start | bytes 3145732
  3.7 4.7 %copy-start.3 = (bf16[64,64,128]{2,1,0:T(8,128)(2,1)S(1)}, bf16[64,64,128]{2,1,0:T(8,128)(2,1)}, u32[]{:S(2)}) copy-start(bf16[64,64,128]{2,1,0:T(8,128)(2,1)} %refs_3_.1) | copy-start | bytes 3145732
  3.7 4.7 %copy-start.5 = (s32[4,8,64,128]{3,2,1,0:T(8,128)S(1)}, s32[4,8,64,128]{3,2,1,0:T(8,128)}, u32[]{:S(2)}) copy-start(s32[4,8,64,128]{3,2,1,0:T(8,128)} %refs_4_.1) | copy-start | bytes 3145732
  5.4 8.4 %collective-permute-start.2 = (bf16[4,144,128]{2,1,0:T(8,128)(2,1)S(1)}, bf16[4,144,128]{2,1,0:T(8,128)(2,1)S(1)}, u32[]{:S(2)}, u32[]{:S(2)}) collective-permute-start(bf16[4,144,128]{2,1,0:T(8,128)(2,1)S(1)} %get-tuple-element.11), channel_id=1, source_target_pairs={{0,1},{1,0},{2,3},{3,2},{4,5},{5,4},{6,7},{7,6},{8,9},{9,8},{10,11... | collective-permute-start | bytes 442376 | tf_op jit(solution)/shard_map/ppermute | solution.py:274
  9.0 7.6 %copy-start.6 = (f32[4,4]{1,0:T(4,128)S(1)}, f32[4,4]{1,0:T(4,128)}, u32[]{:S(2)}) copy-start(f32[4,4]{1,0:T(4,128)} %refs_1_.1) | copy-start | bytes 196
  9.0 4.7 %collective-permute-start = (bf16[4,144,128]{2,1,0:T(8,128)(2,1)S(1)}, bf16[4,144,128]{2,1,0:T(8,128)(2,1)S(1)}, u32[]{:S(2)}, u32[]{:S(2)}) collective-permute-start(bf16[4,144,128]{2,1,0:T(8,128)(2,1)S(1)} %get-tuple-element.9), channel_id=1, source_target_pairs={{0,2},{2,0},{4,6},{6,4},{8,10},{10,8},{12,14},{14,12},{16,18},{18,... | collective-permute-start | bytes 442376 | tf_op jit(solution)/shard_map/ppermute | solution.py:274
  9.0 7.5 %collective-permute-start.1 = (bf16[4,144,128]{2,1,0:T(8,128)(2,1)S(1)}, bf16[4,144,128]{2,1,0:T(8,128)(2,1)S(1)}, u32[]{:S(2)}, u32[]{:S(2)}) collective-permute-start(bf16[4,144,128]{2,1,0:T(8,128)(2,1)S(1)} %get-tuple-element.10), channel_id=1, source_target_pairs={{0,30},{2,4},{4,2},{6,8},{8,6},{10,12},{12,10},{14,16},{16,14},{18... | collective-permute-start | bytes 442376 | tf_op jit(solution)/shard_map/ppermute | solution.py:274

commit v4 on v3

v4 whole, which is shorter than its diff:
```python
import math

import jax
import jax.numpy as jnp
from jax import lax
from jax.experimental import pallas as pl
from jax.experimental.pallas import tpu as pltpu
from jax.sharding import PartitionSpec as P


OPS = 4
RANGE = 4
TAPS = 2 * RANGE
EVEN = tuple(a for a in range(OPS) if a % 2 == 0)
ODD = tuple(a for a in range(OPS) if a % 2 == 1)
SUB = 8
LANES = 128
VMEM = pltpu.VMEM
F32 = jnp.float32
BF16 = jnp.bfloat16
INNER_BODY = 4
MAIN_BODY = 8
VMEM_LIMIT = 24 * 1024 * 1024


def lane_index(shape):
    return lax.broadcasted_iota(jnp.int32, shape, len(shape) - 1)


def pack_kernel(parity, hop, right, left, bonds, near, far, side, own, value, coef, vectors, bits, flat, head, tail, sems):
    count, rows, cols = right.shape
    even = parity[0] == 0
    group = LANES // TAPS
    pitch = rows + 1
    batch = 2 * SUB
    batches = count // batch

    copies = []
    for which, ref in enumerate((right, left)):
        for n in range(batches):
            copies.append((ref.at[pl.ds(n * batch, batch)], vectors.at[which, pl.ds(n * batch, batch)]))
    for a in ODD + EVEN:
        copies.append((bonds.at[a], bits.at[a]))
    copies = [pltpu.make_async_copy(src, dst, sems.at[n]) for n, (src, dst) in enumerate(copies)]
    for copy in copies:
        copy.start()

    lane = lane_index((batch, cols)) // TAPS

    def pack(at, flat):
        for tile in range(rows // group):
            total = jnp.zeros((batch, cols), F32)
            for r in range(group):
                row = tile * group + r
                strip = jnp.concatenate(
                    [flat[pl.ds(half * SUB * pitch + row, SUB, stride=pitch), :] for half in range(2)], axis=0
                )
                total = jnp.where(lane == r, pltpu.roll(strip, (RANGE + TAPS * r) % LANES, 1), total)
            side[tile, at : at + batch, :] = total.astype(BF16)

    def send(at):
        for row in range(RANGE):
            def strip(ref, offset):
                parts = [ref[pl.ds((at + half * SUB) * SUB + offset, SUB, stride=SUB), :] for half in range(2)]
                return jnp.concatenate(parts, axis=0)

            low = strip(head, row)
            high = strip(tail, SUB - RANGE + row)
            near[row, at : at + batch, :] = jnp.where(even, high, low).astype(BF16)
            far[row, at : at + batch, :] = jnp.where(even, low, high).astype(BF16)

    for which in range(2):
        for n in range(batches):
            copies[which * batches + n].wait()
            at = which * count + n * batch
            for v in range(batch):
                one = vectors[which, n * batch + v].astype(F32)
                start = (n * batch + v) * pitch
                value[which, start : start + rows, :] = one
                head[(at + v) * SUB : (at + v + 1) * SUB, :] = one[:SUB]
                tail[(at + v) * SUB : (at + v + 1) * SUB, :] = one[rows - SUB :]
            pack(at, value.at[which, pl.ds(n * batch * pitch, batch * pitch)])
            send(at)
    at = 2 * count
    for n, a in enumerate(ODD + EVEN):
        copies[2 * batches + n].wait()
        for index in range(TAPS):
            scale = hop[a, index % RANGE] * (1.0 if index < RANGE else -1.0)
            sign = (2 * bits[a, index] - 1).astype(F32)
            coef[a * TAPS + index] = sign * scale
            if a in ODD:
                t = ODD.index(a) * TAPS + index
                flat[t * pitch : t * pitch + rows, :] = sign
            else:
                t = at + EVEN.index(a) * TAPS + index
                head[t * SUB : (t + 1) * SUB, :] = sign[:SUB]
                tail[t * SUB : (t + 1) * SUB, :] = sign[rows - SUB :]
    pack(at, flat)
    send(at)
    own[...] = side[:, at:, :]


def along_rows(which, value_at, factor_at):
    totals = {}
    for index in range(TAPS):
        step = (index % RANGE + 1) * (1 if index < RANGE else -1) * (1 if which == 0 else -1)
        moved = value_at(step)
        for a in EVEN:
            term = factor_at(a, index) * moved
            totals[a] = term if index == 0 else totals[a] + term
    return totals


def factor_row(which, row, index):
    step = index % RANGE + 1
    return row if which == 0 else row + (-step if index < RANGE else step)


def inner_kernel(value, coef, inner, along):
    _, rows, count, _ = along.shape
    cols = coef.shape[2]
    pitch = rows + 1
    period = 2 * TAPS

    tile = (period, cols)
    gap = (lane_index(tile) - lax.broadcasted_iota(jnp.int32, tile, 0)) % period
    near_diagonal = lane_index((cols, cols)) - lax.broadcasted_iota(jnp.int32, (cols, cols), 0)
    within = jnp.where((near_diagonal >= -TAPS) & (near_diagonal < TAPS), 1.0, 0.0).astype(BF16)

    def matrices(row):
        pieces = {}
        for a in ODD:
            total = jnp.zeros(tile, F32)
            for k in range(1, RANGE + 1):
                total = jnp.where(gap == period - k, coef[a * TAPS + k - 1, pl.ds(row, period, stride=0), :], total)
                total = jnp.where(gap == k, coef[a * TAPS + RANGE + k - 1, pl.ds(row, period, stride=0), :], total)
            high = total.astype(BF16)
            low = (total - high.astype(F32)).astype(BF16)
            for part, piece in enumerate((high, low)):
                pieces[part, a] = jnp.concatenate([piece] * (cols // period), axis=0) * within
        right_side = jnp.concatenate([jnp.concatenate([pieces[part, a] for a in ODD], axis=1) for part in range(2)], axis=0)
        left_side = jnp.concatenate([jnp.concatenate([pieces[part, a] for part in range(2)], axis=1) for a in ODD], axis=0)
        return right_side, left_side

    def strip(which, g, row):
        return value[which, pl.ds(g * SUB * pitch + row, SUB, stride=pitch), :]

    def columns(row):
        bands = matrices(row)
        for which in range(2):
            middle = jnp.concatenate([strip(which, g, row) for g in range(count // SUB)], axis=0).astype(BF16)
            middle = jnp.concatenate([middle, middle], axis=1)
            dims = (((1,), (which,)), ((), ()))
            along[which, row] = lax.dot_general(middle, bands[which], dims, preferred_element_type=F32)

    def lines(row):
        for which in range(2):
            factors = {}
            for a in EVEN:
                for index in range(TAPS):
                    factors[a, index] = coef[a * TAPS + index, pl.ds(factor_row(which, row, index), SUB, stride=0), :]
            for pair in range(count // (2 * SUB)):
                halves = [
                    along_rows(which, lambda step, g=2 * pair + half: strip(which, g, row + step), lambda a, index: factors[a, index])
                    for half in range(2)
                ]
                for o, a in enumerate(EVEN):
                    at = o * count + pair * 2 * SUB
                    inner[which, row, at : at + 2 * SUB, :] = jnp.concatenate([half[a] for half in halves], axis=0).astype(BF16)

    @pl.loop(0, RANGE // 2)
    def _(n):
        for one in range(2):
            columns(2 * n + one)
            columns(rows - RANGE + 2 * n + one)

    @pl.loop(0, (rows - 2 * RANGE) // INNER_BODY)
    def _(step):
        for n in range(INNER_BODY):
            row = RANGE + step * INNER_BODY + n
            columns(row)
            lines(row)


def main_kernel(widths, parity, hop, coef, value, inner, along, near, far, side, own, out, band, near_ends, ends, acc):
    _, rows, count, _ = along.shape
    cols = coef.shape[2]
    pitch = rows + 1
    even = parity[0] == 0
    group = LANES // TAPS

    def scale_of(a, index):
        return hop[a, index % RANGE] * (1.0 if index < RANGE else -1.0)

    def outer(slab, row):
        low = jnp.where(even, far[row, slab, :].astype(F32), near[row, slab, :].astype(F32))
        high = jnp.where(even, near[row, slab, :].astype(F32), far[row, slab, :].astype(F32))
        return low, high

    for row in range(RANGE):
        low, high = outer(slice(2 * count, 2 * count + 2 * SUB), row)
        for slot in range(len(EVEN) * TAPS):
            a, index = EVEN[slot // TAPS], slot % TAPS
            source = low if index < RANGE else high
            near_ends[slot, row : row + 1, :] = source[slot : slot + 1] * scale_of(a, index)

    for end in range(2):
        for n in range(RANGE):
            row = n if end == 0 else rows - RANGE + n
            for which in range(2):
                def value_at(step, base):
                    at = row + step
                    slab = slice(which * count + base, which * count + base + 2 * SUB)
                    if at < 0:
                        return outer(slab, at + RANGE)[0]
                    if at >= rows:
                        return outer(slab, at - rows)[1]
                    parts = [value[which, pl.ds((base + half * SUB) * pitch + at, SUB, stride=pitch), :] for half in range(2)]
                    return jnp.concatenate(parts, axis=0)

                def factor_at(a, index):
                    at = factor_row(which, row, index)
                    if 0 <= at < rows:
                        one = coef[a * TAPS + index, at : at + 1, :]
                    else:
                        at = at + RANGE if at < 0 else at - rows
                        one = near_ends[EVEN.index(a) * TAPS + index, at : at + 1, :]
                    return jnp.broadcast_to(one, (2 * SUB, cols))

                for base in range(0, count, 2 * SUB):
                    totals = along_rows(which, lambda step, base=base: value_at(step, base), factor_at)
                    for o, a in enumerate(EVEN):
                        at = o * count + base
                        ends[which, end * RANGE + n, at : at + 2 * SUB, :] = totals[a].astype(BF16)

    tile_shape = (count, cols)
    spot = lane_index((1, cols)) % TAPS
    spots = lane_index(tile_shape) % TAPS
    for tile in range(rows // group):
        mine = own[tile].astype(F32)
        theirs = side[tile, 2 * count :, :].astype(F32)
        for which in range(2):
            packed = side[tile, which * count : (which + 1) * count, :].astype(F32)
            total = {}
            for k in range(1, RANGE + 1):
                moved = jnp.where(spots < RANGE, pltpu.roll(packed, LANES - k, 1), pltpu.roll(packed, k, 1))
                for a in ODD:
                    slot = ODD.index(a) * TAPS + k - 1
                    if which == 0:
                        tops, bottoms = mine[slot : slot + 1], mine[slot + RANGE : slot + RANGE + 1]
                        weight = jnp.where(spot < RANGE, tops * scale_of(a, k - 1), bottoms * scale_of(a, RANGE + k - 1))
                    else:
                        tops = pltpu.roll(theirs, LANES - k, 1)[slot + RANGE : slot + RANGE + 1]
                        bottoms = pltpu.roll(theirs, k, 1)[slot : slot + 1]
                        weight = jnp.where(spot < RANGE, tops * scale_of(a, RANGE + k - 1), bottoms * scale_of(a, k - 1))
                    valid = ((spot < RANGE) & (spot + k >= RANGE)) | ((spot >= RANGE) & (spot - k < RANGE))
                    term = jnp.where(valid, weight, 0.0) * moved
                    total[a] = term if k == 1 else total[a] + term
            for a in ODD:
                band[which, ODD.index(a), tile] = total[a]

    acc[...] = jnp.zeros_like(acc)
    rim_lane = (lane_index(tile_shape) < RANGE) | (lane_index(tile_shape) >= cols - RANGE)

    def results(row, even_of):
        found = []
        tile = row // group
        turn = (2 * LANES - RANGE - TAPS * (row % group)) % LANES
        for which in range(2):
            both = along[which, row]
            done = {a: even_of(which)[EVEN.index(a) * count : (EVEN.index(a) + 1) * count] for a in EVEN}
            for o, a in enumerate(ODD):
                beyond = jnp.where(rim_lane, pltpu.roll(band[which, o, tile], turn, 1), 0.0)
                done[a] = (both[:, o * cols : (o + 1) * cols] + beyond).astype(BF16)
            found.append(jnp.concatenate([done[a] for a in range(OPS)], axis=0))
        return found

    def accumulate(pairs):
        for pair in pairs:
            found = [results(*one) for one in pair]
            first = jnp.concatenate([one[0] for one in found], axis=1)
            back = jnp.concatenate([one[1] for one in found], axis=1)
            acc[...] += lax.dot_general(back, first, (((1,), (1,)), ((), ())), preferred_element_type=F32)

    def end_row(n):
        return (n if n < RANGE else rows - 2 * RANGE + n), lambda which: ends[which, n]

    accumulate([[end_row(n), end_row(n + 1)] for n in range(0, 2 * RANGE, 2)])

    @pl.loop(0, (rows - 2 * RANGE) // MAIN_BODY)
    def _(step):
        def inner_row(n):
            row = RANGE + step * MAIN_BODY + n
            return row, lambda which: inner[which, row]

        accumulate([[inner_row(n), inner_row(n + 1)] for n in range(0, MAIN_BODY, 2)])

    parts_left, parts_right = widths
    per_left, per_right = count // parts_left, count // parts_right
    size = OPS * count

    def order(per, dim):
        new = lax.broadcasted_iota(jnp.int32, (size, size), dim)
        old = lax.broadcasted_iota(jnp.int32, (size, size), 1 - dim)
        part, rest = new // (OPS * per), new % (OPS * per)
        return jnp.where(old == (rest // per) * count + part * per + rest % per, 1.0, 0.0).astype(BF16)

    moved = jnp.dot(order(per_left, 0), acc[...].astype(BF16), preferred_element_type=F32).astype(BF16)
    moved = jnp.dot(moved, order(per_right, 1), preferred_element_type=F32).astype(BF16)
    if out.ndim == 2:
        out[...] = moved
    else:
        width = OPS * per_right
        for d in range(parts_left * parts_right):
            w, r = divmod(d, parts_right)
            out[d] = moved[w * OPS * per_left : (w + 1) * OPS * per_left, r * width : (r + 1) * width]


def sum_kernel(factor, got, out):
    total = jnp.sum(got[...].astype(F32), axis=0) * factor
    per_left, per_right = out.shape[1], out.shape[2]
    for a in range(OPS):
        for b in range(OPS):
            out[a * OPS + b] = total[a * per_left : (a + 1) * per_left, b * per_right : (b + 1) * per_right]


def swap(array, axis, pairs):
    return lax.ppermute(array, axis, pairs)


def on_device(left, right, bond_signs, hop):
    count, rows, cols = right.shape
    wide, narrow = lax.axis_size("wide"), lax.axis_size("narrow")
    edge_rows = 2 * count + len(EVEN) * TAPS
    side_rows = 2 * count + len(ODD) * TAPS
    tiles = rows * TAPS // LANES
    parity = (lax.axis_index("wide") % 2).astype(jnp.int32).reshape(1)
    smem = pl.BlockSpec(memory_space=pltpu.SMEM)
    vmem = pl.BlockSpec(memory_space=pltpu.VMEM)
    params = pltpu.CompilerParams(vmem_limit_bytes=VMEM_LIMIT)

    hbm = pl.BlockSpec(memory_space=pltpu.HBM)

    near, far, side, own, value, coef = pl.pallas_call(
        pack_kernel,
        out_shape=(
            jax.ShapeDtypeStruct((RANGE, edge_rows, cols), BF16),
            jax.ShapeDtypeStruct((RANGE, edge_rows, cols), BF16),
            jax.ShapeDtypeStruct((tiles, side_rows, cols), BF16),
            jax.ShapeDtypeStruct((tiles, side_rows - 2 * count, cols), BF16),
            jax.ShapeDtypeStruct((2, count * (rows + 1), cols), F32),
            jax.ShapeDtypeStruct((OPS * TAPS, rows, cols), F32),
        ),
        in_specs=[smem, smem, hbm, hbm, hbm],
        out_specs=(vmem,) * 6,
        scratch_shapes=[
            VMEM((2, count, rows, cols), BF16),
            VMEM((OPS, TAPS, rows, cols), jnp.int32),
            VMEM((2 * SUB * (rows + 1), cols), F32),
            VMEM((edge_rows * SUB, cols), F32),
            VMEM((edge_rows * SUB, cols), F32),
            pltpu.SemaphoreType.DMA((2 * (count // (2 * SUB)) + OPS,)),
        ],
        compiler_params=params,
        name="pack",
    )(parity, hop, *(pltpu.with_memory_space_constraint(one, pltpu.HBM) for one in (right, left, bond_signs)))
    inner, along = pl.pallas_call(
        inner_kernel,
        out_shape=(
            jax.ShapeDtypeStruct((2, rows, len(EVEN) * count, cols), BF16),
            jax.ShapeDtypeStruct((2, rows, count, len(ODD) * cols), F32),
        ),
        in_specs=[vmem, vmem],
        out_specs=(vmem,) * 2,
        compiler_params=params,
        name="interior",
    )(value, coef)

    far = swap(far, "wide", [(i, (i + 1) % wide if i % 2 else (i - 1) % wide) for i in range(wide)])
    near = swap(near, "wide", [(i, i ^ 1) for i in range(wide)])
    if narrow == 2:
        side = swap(side, "narrow", [(0, 1), (1, 0)])
    else:
        before = swap(side, "narrow", [(i, (i + 1) % narrow) for i in range(narrow)])
        after = swap(side, "narrow", [((i + 1) % narrow, i) for i in range(narrow)])
        side = jnp.where(lane_index(side.shape) % TAPS < RANGE, before, after)

    per_left, per_right = count // wide, count // narrow
    size = OPS * count
    direct = (OPS * per_right) % LANES == 0 and (OPS * per_left) % 16 == 0
    blocked = (wide * narrow, OPS * per_left, OPS * per_right)
    partial = pl.pallas_call(
        lambda *refs: main_kernel((wide, narrow), *refs),
        out_shape=jax.ShapeDtypeStruct(blocked if direct else (size, size), BF16),
        in_specs=[smem, smem] + [vmem] * 8,
        out_specs=vmem,
        scratch_shapes=[
            VMEM((2, len(ODD), tiles, count, cols), F32),
            VMEM((len(EVEN) * TAPS, RANGE, cols), F32),
            VMEM((2, 2 * RANGE, len(EVEN) * count, cols), BF16),
            VMEM((size, size), F32),
        ],
        compiler_params=params,
        name="moments",
    )(parity, hop, coef, value, inner, along, near, far, side, own)
    if not direct:
        partial = partial.reshape(wide, OPS * per_left, narrow, OPS * per_right).transpose(0, 2, 1, 3).reshape(blocked)
    got = lax.all_to_all(partial, ("wide", "narrow"), 0, 0, tiled=True)
    factor = 1.0 / math.sqrt(rows * cols * wide * narrow)
    return pl.pallas_call(
        lambda *refs: sum_kernel(factor, *refs),
        out_shape=jax.ShapeDtypeStruct((OPS * OPS, per_left, per_right), F32),
        in_specs=[vmem],
        out_specs=vmem,
        name="total",
    )(got)


def solution(mesh):
    in_specs = (
        P(None, "wide", "narrow"),
        P(None, "wide", "narrow"),
        P(None, None, "wide", "narrow"),
        P(),
    )
    out_specs = P(None, "wide", "narrow")

    return jax.shard_map(on_device, mesh=mesh, in_specs=in_specs, out_specs=out_specs, check_vma=False)
```

time: 41.6 us -> 39.1 us (0.940)
  Pallas kernels: 13.7 us -> 19.5 us
  local copies, waits for them, and re-layouts: 3.69 us -> 0.68 us
  waiting for transfers between devices: 2.82 us -> 0.01 us
  blocking collectives: 13.3 us -> 11 us
    pallas_call x2, Pallas kernels: 2.22 us -> 11.9 us  [the longest x1 8.48 us: on_device(): pl.pallas_call(inner_kernel, out_shape=(jax.ShapeDtypeStruct((2, rows, le...]
    pallas_call x1, Pallas kernels: 9.81 us -> 5.98 us  [on_device(): pl.pallas_call(lambda *refs: main_kernel((wide, narrow), *refs), out_shap...]
    unnamed x14 -> x2, local copies, waits for them, and re-layouts: 3.69 us -> 0.68 us
    ppermute x3, waiting for transfers between devices: 2.82 us -> 0.01 us  [swap(): return lax.ppermute(array, axis, pairs)]
    all_to_all x1, blocking collectives: 13.3 us -> 11 us  [on_device(): got = lax.all_to_all(partial, ('wide', 'narrow'), 0, 0, tiled=True)]
  transfers between devices with their start and end apart: 3 -> 3, of which waited for: 1 -> 0; matrix products, arithmetic and copies ran while one was open for 0% -> 0% of each run, Pallas kernels for 1% -> 22%
where the time goes in v4:
time: 39.1 us; the launch traced here: 38.9 us
  Pallas kernels  19.5 us (50%)
  blocking collectives  11 us (28%)
  starting transfers between devices  7.7 us (20%)
  local copies, waits for them, and re-layouts  0.68 us (2%)
    all_to_all x1, blocking collectives, on_device(): got = lax.all_to_all(partial, ('wide', 'narrow'), 0, 0, tiled=True)  11 us
    pallas_call x1, Pallas kernels, on_device(): pl.pallas_call(inner_kernel, out_shape=(jax.ShapeDtypeStruct((2, rows, le...  8.48 us
    ppermute x3, starting transfers between devices, swap(): return lax.ppermute(array, axis, pairs)  7.7 us
    pallas_call x1, Pallas kernels, on_device(): pl.pallas_call(lambda *refs: main_kernel((wide, narrow), *refs), out_shap...  5.98 us
    pallas_call x1, Pallas kernels, on_device(): pl.pallas_call(pack_kernel, out_shape=(jax.ShapeDtypeStruct((RANGE, edge_...  3.43 us
    pallas_call x1, Pallas kernels, on_device(): pl.pallas_call(lambda *refs: sum_kernel(factor, *refs), out_shape=jax.Sha...  1.63 us
  transfers between devices with their start and end apart: 3, of which 0 were waited for; matrix products, arithmetic and copies ran while one was open for 0% of the time, Pallas kernels for 22%

profile of v4, /device:TPU:0, one launch (start us, length us, event | category | flops | bytes accessed | tf_op | source)
XLA Modules:
  0.0 38.9 jit_solution(14979455146859074465)
XLA Ops:
  0.0 0.0 copy-start
  0.0 0.7 %copy-done = f32[4,4]{1,0:T(4,128)S(1)} copy-done((f32[4,4]{1,0:T(4,128)S(1)}, f32[4,4]{1,0:T(4,128)}, u32[]{:S(2)}) %copy-start) | copy-done | bytes 88
  0.7 3.4 %pack.1 = (bf16[4,144,128]{2,1,0:T(8,128)(2,1)S(1)}, bf16[4,144,128]{2,1,0:T(8,128)(2,1)S(1)}, bf16[4,144,128]{2,1,0:T(8,128)(2,1)S(1)}, bf16[4,16,128]{2,1,0:T(...) custom-call(s32[1]{0:T(128)} %bitcast.parity.refs_0_, f32[4,4]{1,0:T(4,128)S(1)} %copy-done, ...), custom_call_target="tpu_custom_call" | custom-call | tf_op jit(solution)/shard_map/pack/pallas_call | solution.py:344
  4.1 0.6 %collective-permute-start = (bf16[4,144,128]{2,1,0:T(8,128)(2,1)S(1)}, bf16[4,144,128]{2,1,0:T(8,128)(2,1)S(1)}, u32[]{:S(2)}, u32[]{:S(2)}) collective-permute-start(bf16[4,144,128]{2,1,0:T(8,128)(2,1)S(1)} %get-tuple-element.17), channel_id=1, source_target_pairs={{0,2},{2,0},{4,6},{6,4},{8,10},{10,8},{12,14},{14,12},{16,18},{18,... | collective-permute-start | bytes 442376 | tf_op jit(solution)/shard_map/ppermute | solution.py:328
  4.7 5.7 %collective-permute-start.1 = (bf16[4,144,128]{2,1,0:T(8,128)(2,1)S(1)}, bf16[4,144,128]{2,1,0:T(8,128)(2,1)S(1)}, u32[]{:S(2)}, u32[]{:S(2)}) collective-permute-start(bf16[4,144,128]{2,1,0:T(8,128)(2,1)S(1)} %get-tuple-element.18), channel_id=1, source_target_pairs={{0,30},{2,4},{4,2},{6,8},{8,6},{10,12},{12,10},{14,16},{16,14},{18... | collective-permute-start | bytes 442376 | tf_op jit(solution)/shard_map/ppermute | solution.py:328
  10.3 1.5 %collective-permute-start.2 = (bf16[4,144,128]{2,1,0:T(8,128)(2,1)S(1)}, bf16[4,144,128]{2,1,0:T(8,128)(2,1)S(1)}, u32[]{:S(2)}, u32[]{:S(2)}) collective-permute-start(bf16[4,144,128]{2,1,0:T(8,128)(2,1)S(1)} %get-tuple-element.19), channel_id=1, source_target_pairs={{0,1},{1,0},{2,3},{3,2},{4,5},{5,4},{6,7},{7,6},{8,9},{9,8},{10,11... | collective-permute-start | bytes 442376 | tf_op jit(solution)/shard_map/ppermute | solution.py:328
  11.8 8.5 %interior.1 = (bf16[2,64,128,128]{3,2,1,0:T(8,128)(2,1)S(1)}, f32[2,64,64,256]{3,2,1,0:T(8,128)S(1)}) custom-call(f32[2,4160,128]{2,1,0:T(8,128)S(1)} %get-tuple-element.14.value.refs_3_, f32[32,64,128]{2,1,0:T(8,128)S(1)} %get-tuple-element.13.coef.refs_2_), custom_call_target="tpu_custom_call" | custom-call | tf_op jit(solution)/shard_map/interior/pallas_call | solution.py:367
  20.3 0.0 collective-permute-done.refs_6_
  20.3 0.0 collective-permute-done.1.refs_7_
  20.3 0.0 collective-permute-done.2.refs_8_
  20.3 6.0 %moments.1 = bf16[32,16,128]{2,1,0:T(8,128)(2,1)S(1)} custom-call(s32[1]{0:T(128)} %bitcast.parity.refs_0_, f32[4,4]{1,0:T(4,128)S(1)} %copy-done, f32[32,64,128]{2,1,0:T(8,128)S(1)} %get-tuple-element.13.coef.refs_2_, f32[2,4160,128]{2,1,0:T(8,128)S(1)} %get-tuple-element.14.value.refs_3_, bf16[2,64,128,128]{3,2,1,0:T(8,128)(2,1)S(1)} %get-tuple-element.15.refs_4_, ...), custom_call_target="tpu_custom_call" | custom-call | tf_op jit(solution)/shard_map/moments/pallas_call | solution.py:392
  26.3 11.0 %all_to_all.5.refs_0_ = bf16[32,16,128]{2,1,0:T(8,128)(2,1)} all-to-all(bf16[32,16,128]{2,1,0:T(8,128)(2,1)S(1)} %moments.1), channel_id=1, replica_groups=mesh['wide'=16,'narrow'=2] {'wide','narrow'}, dimensions={0} | all-to-all | bytes 262144 | tf_op jit(solution)/shard_map/all_to_all | solution.py:408
  37.3 1.6 %total.1 = f32[16,4,32]{2,1,0:T(4,128)} custom-call(bf16[32,16,128]{2,1,0:T(8,128)(2,1)} %all_to_all.5.refs_0_), custom_call_target="tpu_custom_call" | custom-call | tf_op jit(solution)/shard_map/total/pallas_call | solution.py:410
Async XLA Ops:
  0.0 0.7 %copy-start = (f32[4,4]{1,0:T(4,128)S(1)}, f32[4,4]{1,0:T(4,128)}, u32[]{:S(2)}) copy-start(f32[4,4]{1,0:T(4,128)} %refs_1_.1) | copy-start | bytes 196
  4.1 16.2 %collective-permute-start = (bf16[4,144,128]{2,1,0:T(8,128)(2,1)S(1)}, bf16[4,144,128]{2,1,0:T(8,128)(2,1)S(1)}, u32[]{:S(2)}, u32[]{:S(2)}) collective-permute-start(bf16[4,144,128]{2,1,0:T(8,128)(2,1)S(1)} %get-tuple-element.17), channel_id=1, source_target_pairs={{0,2},{2,0},{4,6},{6,4},{8,10},{10,8},{12,14},{14,12},{16,18},{18,... | collective-permute-start | bytes 442376 | tf_op jit(solution)/shard_map/ppermute | solution.py:328
  4.7 15.6 %collective-permute-start.1 = (bf16[4,144,128]{2,1,0:T(8,128)(2,1)S(1)}, bf16[4,144,128]{2,1,0:T(8,128)(2,1)S(1)}, u32[]{:S(2)}, u32[]{:S(2)}) collective-permute-start(bf16[4,144,128]{2,1,0:T(8,128)(2,1)S(1)} %get-tuple-element.18), channel_id=1, source_target_pairs={{0,30},{2,4},{4,2},{6,8},{8,6},{10,12},{12,10},{14,16},{16,14},{18... | collective-permute-start | bytes 442376 | tf_op jit(solution)/shard_map/ppermute | solution.py:328
  10.3 10.0 %collective-permute-start.2 = (bf16[4,144,128]{2,1,0:T(8,128)(2,1)S(1)}, bf16[4,144,128]{2,1,0:T(8,128)(2,1)S(1)}, u32[]{:S(2)}, u32[]{:S(2)}) collective-permute-start(bf16[4,144,128]{2,1,0:T(8,128)(2,1)S(1)} %get-tuple-element.19), channel_id=1, source_target_pairs={{0,1},{1,0},{2,3},{3,2},{4,5},{5,4},{6,7},{7,6},{8,9},{9,8},{10,11... | collective-permute-start | bytes 442376 | tf_op jit(solution)/shard_map/ppermute | solution.py:328

commit v5 on v4

--- a/solution.py
+++ b/solution.py
@@ -18,8 +18,8 @@
 VMEM = pltpu.VMEM
 F32 = jnp.float32
 BF16 = jnp.bfloat16
-INNER_BODY = 4
-MAIN_BODY = 8
+INNER_BODY = 14
+MAIN_BODY = 28
 VMEM_LIMIT = 24 * 1024 * 1024
 
 
@@ -27,7 +27,7 @@
     return lax.broadcasted_iota(jnp.int32, shape, len(shape) - 1)
 
 
-def pack_kernel(parity, hop, right, left, bonds, near, far, side, own, value, coef, vectors, bits, flat, head, tail, sems):
+def pack_kernel(parity, hop_far, right, left, bonds, near, far, side, own, value, coef, hop, vectors, bits, flat, head, tail, sems):
     count, rows, cols = right.shape
     even = parity[0] == 0
     group = LANES // TAPS
@@ -41,6 +41,7 @@
             copies.append((ref.at[pl.ds(n * batch, batch)], vectors.at[which, pl.ds(n * batch, batch)]))
     for a in ODD + EVEN:
         copies.append((bonds.at[a], bits.at[a]))
+    copies.append((hop_far, hop))
     copies = [pltpu.make_async_copy(src, dst, sems.at[n]) for n, (src, dst) in enumerate(copies)]
     for copy in copies:
         copy.start()
@@ -71,7 +72,8 @@
 
     for which in range(2):
         for n in range(batches):
-            copies[which * batches + n].wait()
+            for m in range(n, n + 4 if n % 4 == 0 else n):
+                copies[which * batches + m].wait()
             at = which * count + n * batch
             for v in range(batch):
                 one = vectors[which, n * batch + v].astype(F32)
@@ -82,6 +84,7 @@
             pack(at, value.at[which, pl.ds(n * batch * pitch, batch * pitch)])
             send(at)
     at = 2 * count
+    copies[-1].wait()
     for n, a in enumerate(ODD + EVEN):
         copies[2 * batches + n].wait()
         for index in range(TAPS):
@@ -351,19 +354,20 @@
             jax.ShapeDtypeStruct((2, count * (rows + 1), cols), F32),
             jax.ShapeDtypeStruct((OPS * TAPS, rows, cols), F32),
         ),
-        in_specs=[smem, smem, hbm, hbm, hbm],
+        in_specs=[smem, hbm, hbm, hbm, hbm],
         out_specs=(vmem,) * 6,
         scratch_shapes=[
+            pltpu.SMEM((OPS, RANGE), F32),
             VMEM((2, count, rows, cols), BF16),
             VMEM((OPS, TAPS, rows, cols), jnp.int32),
             VMEM((2 * SUB * (rows + 1), cols), F32),
             VMEM((edge_rows * SUB, cols), F32),
             VMEM((edge_rows * SUB, cols), F32),
-            pltpu.SemaphoreType.DMA((2 * (count // (2 * SUB)) + OPS,)),
+            pltpu.SemaphoreType.DMA((2 * (count // (2 * SUB)) + OPS + 1,)),
         ],
         compiler_params=params,
         name="pack",
-    )(parity, hop, *(pltpu.with_memory_space_constraint(one, pltpu.HBM) for one in (right, left, bond_signs)))
+    )(parity, *(pltpu.with_memory_space_constraint(one, pltpu.HBM) for one in (hop, right, left, bond_signs)))
     inner, along = pl.pallas_call(
         inner_kernel,
         out_shape=(
@@ -412,6 +416,7 @@
         out_shape=jax.ShapeDtypeStruct((OPS * OPS, per_left, per_right), F32),
         in_specs=[vmem],
         out_specs=vmem,
+        compiler_params=params,
         name="total",
     )(got)
 

time: 39.1 us -> 34 us (0.87)
  Pallas kernels: 19.5 us -> 15.8 us
  blocking collectives: 11 us -> 10.3 us
  local copies, waits for them, and re-layouts: 0.68 us -> 0.01 us
    pallas_call x1, Pallas kernels: 5.98 us -> 4.93 us  [on_device(): pl.pallas_call(lambda *refs: main_kernel((wide, narrow), *refs), out_shap...]
    pallas_call x1, Pallas kernels: 8.48 us -> 7.47 us  [on_device(): pl.pallas_call(inner_kernel, out_shape=(jax.ShapeDtypeStruct((2, rows, le...]
    pallas_call x1, Pallas kernels: 1.63 us -> 0.72 us  [on_device(): pl.pallas_call(lambda *refs: sum_kernel(factor, *refs), out_shape=jax.Sha...]
    pallas_call x1, Pallas kernels: 3.43 us -> 2.66 us  [on_device(): pl.pallas_call(pack_kernel, out_shape=(jax.ShapeDtypeStruct((RANGE, edge_...]
    all_to_all x1, blocking collectives: 11 us -> 10.3 us  [on_device(): got = lax.all_to_all(partial, ('wide', 'narrow'), 0, 0, tiled=True)]
    unnamed x2, local copies, waits for them, and re-layouts: 0.68 us -> 0.01 us
where the time goes in v5:
time: 34 us; the launch traced here: 33.8 us
  Pallas kernels  15.8 us (46%)
  blocking collectives  10.3 us (30%)
  starting transfers between devices  7.7 us (23%)
    all_to_all x1, blocking collectives, on_device(): got = lax.all_to_all(partial, ('wide', 'narrow'), 0, 0, tiled=True)  10.3 us
    ppermute x3, starting transfers between devices, swap(): return lax.ppermute(array, axis, pairs)  7.7 us
    pallas_call x1, Pallas kernels, on_device(): pl.pallas_call(inner_kernel, out_shape=(jax.ShapeDtypeStruct((2, rows, le...  7.47 us
    pallas_call x1, Pallas kernels, on_device(): pl.pallas_call(lambda *refs: main_kernel((wide, narrow), *refs), out_shap...  4.93 us
    pallas_call x1, Pallas kernels, on_device(): pl.pallas_call(pack_kernel, out_shape=(jax.ShapeDtypeStruct((RANGE, edge_...  2.66 us
    pallas_call x1, Pallas kernels, on_device(): pl.pallas_call(lambda *refs: sum_kernel(factor, *refs), out_shape=jax.Sha...  0.72 us
  transfers between devices with their start and end apart: 3, of which 0 were waited for; matrix products, arithmetic and copies ran while one was open for 0% of the time, Pallas kernels for 22%

profile of v5, /device:TPU:0, one launch (start us, length us, event | category | flops | bytes accessed | tf_op | source)
XLA Modules:
  0.0 33.8 jit_solution(18172186071085198387)
XLA Ops:
  0.0 0.0 copy-start
  0.0 2.7 %pack.1 = (bf16[4,144,128]{2,1,0:T(8,128)(2,1)S(1)}, bf16[4,144,128]{2,1,0:T(8,128)(2,1)S(1)}, bf16[4,144,128]{2,1,0:T(8,128)(2,1)S(1)}, bf16[4,16,128]{2,1,0:T(...) custom-call(s32[1]{0:T(128)} %bitcast.parity.refs_0_, f32[4,4]{1,0:T(4,128)} %refs_1_.1, ...), custom_call_target="tpu_custom_call" | custom-call | tf_op jit(solution)/shard_map/pack/pallas_call | solution.py:347
  2.7 0.6 %collective-permute-start = (bf16[4,144,128]{2,1,0:T(8,128)(2,1)S(1)}, bf16[4,144,128]{2,1,0:T(8,128)(2,1)S(1)}, u32[]{:S(2)}, u32[]{:S(2)}) collective-permute-start(bf16[4,144,128]{2,1,0:T(8,128)(2,1)S(1)} %get-tuple-element.17), channel_id=1, source_target_pairs={{0,2},{2,0},{4,6},{6,4},{8,10},{10,8},{12,14},{14,12},{16,18},{18,... | collective-permute-start | bytes 442376 | tf_op jit(solution)/shard_map/ppermute | solution.py:331
  3.2 5.7 %collective-permute-start.1 = (bf16[4,144,128]{2,1,0:T(8,128)(2,1)S(1)}, bf16[4,144,128]{2,1,0:T(8,128)(2,1)S(1)}, u32[]{:S(2)}, u32[]{:S(2)}) collective-permute-start(bf16[4,144,128]{2,1,0:T(8,128)(2,1)S(1)} %get-tuple-element.18), channel_id=1, source_target_pairs={{0,30},{2,4},{4,2},{6,8},{8,6},{10,12},{12,10},{14,16},{16,14},{18... | collective-permute-start | bytes 442376 | tf_op jit(solution)/shard_map/ppermute | solution.py:331
  8.9 1.5 %collective-permute-start.2 = (bf16[4,144,128]{2,1,0:T(8,128)(2,1)S(1)}, bf16[4,144,128]{2,1,0:T(8,128)(2,1)S(1)}, u32[]{:S(2)}, u32[]{:S(2)}) collective-permute-start(bf16[4,144,128]{2,1,0:T(8,128)(2,1)S(1)} %get-tuple-element.19), channel_id=1, source_target_pairs={{0,1},{1,0},{2,3},{3,2},{4,5},{5,4},{6,7},{7,6},{8,9},{9,8},{10,11... | collective-permute-start | bytes 442376 | tf_op jit(solution)/shard_map/ppermute | solution.py:331
  10.4 7.5 %interior.1 = (bf16[2,64,128,128]{3,2,1,0:T(8,128)(2,1)S(1)}, f32[2,64,64,256]{3,2,1,0:T(8,128)S(1)}) custom-call(f32[2,4160,128]{2,1,0:T(8,128)S(1)} %get-tuple-element.14.value.refs_3_, f32[32,64,128]{2,1,0:T(8,128)S(1)} %get-tuple-element.13.coef.refs_2_), custom_call_target="tpu_custom_call" | custom-call | tf_op jit(solution)/shard_map/interior/pallas_call | solution.py:371
  17.8 0.0 collective-permute-done.refs_6_
  17.9 0.0 collective-permute-done.1.refs_7_
  17.9 0.0 collective-permute-done.2.refs_8_
  17.9 0.0 copy-done
  17.9 4.9 %moments.1 = bf16[32,16,128]{2,1,0:T(8,128)(2,1)S(1)} custom-call(s32[1]{0:T(128)} %bitcast.parity.refs_0_, f32[4,4]{1,0:T(4,128)S(1)} %copy-done, f32[32,64,128]{2,1,0:T(8,128)S(1)} %get-tuple-element.13.coef.refs_2_, f32[2,4160,128]{2,1,0:T(8,128)S(1)} %get-tuple-element.14.value.refs_3_, bf16[2,64,128,128]{3,2,1,0:T(8,128)(2,1)S(1)} %get-tuple-element.15.refs_4_, ...), custom_call_target="tpu_custom_call" | custom-call | tf_op jit(solution)/shard_map/moments/pallas_call | solution.py:396
  22.8 10.3 %all_to_all.5.refs_0_ = bf16[32,16,128]{2,1,0:T(8,128)(2,1)S(1)} all-to-all(bf16[32,16,128]{2,1,0:T(8,128)(2,1)S(1)} %moments.1), channel_id=1, replica_groups=mesh['wide'=16,'narrow'=2] {'wide','narrow'}, dimensions={0} | all-to-all | bytes 262144 | tf_op jit(solution)/shard_map/all_to_all | solution.py:412
  33.1 0.7 %total.1 = f32[16,4,32]{2,1,0:T(4,128)} custom-call(bf16[32,16,128]{2,1,0:T(8,128)(2,1)S(1)} %all_to_all.5.refs_0_), custom_call_target="tpu_custom_call" | custom-call | tf_op jit(solution)/shard_map/total/pallas_call | solution.py:414
Async XLA Ops:
  0.0 17.9 %copy-start = (f32[4,4]{1,0:T(4,128)S(1)}, f32[4,4]{1,0:T(4,128)}, u32[]{:S(2)}) copy-start(f32[4,4]{1,0:T(4,128)} %refs_1_.1) | copy-start | bytes 196
  2.7 15.2 %collective-permute-start = (bf16[4,144,128]{2,1,0:T(8,128)(2,1)S(1)}, bf16[4,144,128]{2,1,0:T(8,128)(2,1)S(1)}, u32[]{:S(2)}, u32[]{:S(2)}) collective-permute-start(bf16[4,144,128]{2,1,0:T(8,128)(2,1)S(1)} %get-tuple-element.17), channel_id=1, source_target_pairs={{0,2},{2,0},{4,6},{6,4},{8,10},{10,8},{12,14},{14,12},{16,18},{18,... | collective-permute-start | bytes 442376 | tf_op jit(solution)/shard_map/ppermute | solution.py:331
  3.2 14.6 %collective-permute-start.1 = (bf16[4,144,128]{2,1,0:T(8,128)(2,1)S(1)}, bf16[4,144,128]{2,1,0:T(8,128)(2,1)S(1)}, u32[]{:S(2)}, u32[]{:S(2)}) collective-permute-start(bf16[4,144,128]{2,1,0:T(8,128)(2,1)S(1)} %get-tuple-element.18), channel_id=1, source_target_pairs={{0,30},{2,4},{4,2},{6,8},{8,6},{10,12},{12,10},{14,16},{16,14},{18... | collective-permute-start | bytes 442376 | tf_op jit(solution)/shard_map/ppermute | solution.py:331
  8.9 9.0 %collective-permute-start.2 = (bf16[4,144,128]{2,1,0:T(8,128)(2,1)S(1)}, bf16[4,144,128]{2,1,0:T(8,128)(2,1)S(1)}, u32[]{:S(2)}, u32[]{:S(2)}) collective-permute-start(bf16[4,144,128]{2,1,0:T(8,128)(2,1)S(1)} %get-tuple-element.19), channel_id=1, source_target_pairs={{0,1},{1,0},{2,3},{3,2},{4,5},{5,4},{6,7},{7,6},{8,9},{9,8},{10,11... | collective-permute-start | bytes 442376 | tf_op jit(solution)/shard_map/ppermute | solution.py:331

commit v6 on v5

--- a/solution.py
+++ b/solution.py
@@ -18,7 +18,8 @@
 VMEM = pltpu.VMEM
 F32 = jnp.float32
 BF16 = jnp.bfloat16
-INNER_BODY = 14
+INNER_BODY = 28
+INNER_LEAD = 6
 MAIN_BODY = 28
 VMEM_LIMIT = 24 * 1024 * 1024
 
@@ -81,7 +82,7 @@
                 value[which, start : start + rows, :] = one
                 head[(at + v) * SUB : (at + v + 1) * SUB, :] = one[:SUB]
                 tail[(at + v) * SUB : (at + v + 1) * SUB, :] = one[rows - SUB :]
-            pack(at, value.at[which, pl.ds(n * batch * pitch, batch * pitch)])
+            pack(at, value.at[which, pl.ds(n * batch * pitch, (batch + SUB) * pitch)])
             send(at)
     at = 2 * count
     copies[-1].wait()
@@ -90,7 +91,7 @@
         for index in range(TAPS):
             scale = hop[a, index % RANGE] * (1.0 if index < RANGE else -1.0)
             sign = (2 * bits[a, index] - 1).astype(F32)
-            coef[a * TAPS + index] = sign * scale
+            coef[a * TAPS + index, :rows, :] = sign * scale
             if a in ODD:
                 t = ODD.index(a) * TAPS + index
                 flat[t * pitch : t * pitch + rows, :] = sign
@@ -171,18 +172,17 @@
                     at = o * count + pair * 2 * SUB
                     inner[which, row, at : at + 2 * SUB, :] = jnp.concatenate([half[a] for half in halves], axis=0).astype(BF16)
 
-    @pl.loop(0, RANGE // 2)
-    def _(n):
-        for one in range(2):
-            columns(2 * n + one)
-            columns(rows - RANGE + 2 * n + one)
-
-    @pl.loop(0, (rows - 2 * RANGE) // INNER_BODY)
+    trips = (rows - 2 * RANGE) // INNER_BODY
+    each = rows // trips
+
+    @pl.loop(0, trips)
     def _(step):
-        for n in range(INNER_BODY):
-            row = RANGE + step * INNER_BODY + n
-            columns(row)
-            lines(row)
+        for n in range(each):
+            columns(step * each + n)
+            if n >= INNER_LEAD:
+                lines(RANGE + step * INNER_BODY + n - INNER_LEAD)
+        for n in range(each - INNER_LEAD, INNER_BODY):
+            lines(RANGE + step * INNER_BODY + n)
 
 
 def main_kernel(widths, parity, hop, coef, value, inner, along, near, far, side, own, out, band, near_ends, ends, acc):
@@ -243,10 +243,10 @@
         mine = own[tile].astype(F32)
         theirs = side[tile, 2 * count :, :].astype(F32)
         for which in range(2):
-            packed = side[tile, which * count : (which + 1) * count, :].astype(F32)
+            packed = side[tile, which * count : (which + 1) * count, :]
             total = {}
             for k in range(1, RANGE + 1):
-                moved = jnp.where(spots < RANGE, pltpu.roll(packed, LANES - k, 1), pltpu.roll(packed, k, 1))
+                moved = jnp.where(spots < RANGE, pltpu.roll(packed, LANES - k, 1).astype(F32), pltpu.roll(packed, k, 1).astype(F32))
                 for a in ODD:
                     slot = ODD.index(a) * TAPS + k - 1
                     if which == 0:
@@ -260,7 +260,7 @@
                     term = jnp.where(valid, weight, 0.0) * moved
                     total[a] = term if k == 1 else total[a] + term
             for a in ODD:
-                band[which, ODD.index(a), tile] = total[a]
+                band[which, ODD.index(a), tile] = total[a].astype(BF16)
 
     acc[...] = jnp.zeros_like(acc)
     rim_lane = (lane_index(tile_shape) < RANGE) | (lane_index(tile_shape) >= cols - RANGE)
@@ -273,7 +273,7 @@
             both = along[which, row]
             done = {a: even_of(which)[EVEN.index(a) * count : (EVEN.index(a) + 1) * count] for a in EVEN}
             for o, a in enumerate(ODD):
-                beyond = jnp.where(rim_lane, pltpu.roll(band[which, o, tile], turn, 1), 0.0)
+                beyond = jnp.where(rim_lane, pltpu.roll(band[which, o, tile], turn, 1).astype(F32), 0.0)
                 done[a] = (both[:, o * cols : (o + 1) * cols] + beyond).astype(BF16)
             found.append(jnp.concatenate([done[a] for a in range(OPS)], axis=0))
         return found
@@ -351,8 +351,8 @@
             jax.ShapeDtypeStruct((RANGE, edge_rows, cols), BF16),
             jax.ShapeDtypeStruct((tiles, side_rows, cols), BF16),
             jax.ShapeDtypeStruct((tiles, side_rows - 2 * count, cols), BF16),
-            jax.ShapeDtypeStruct((2, count * (rows + 1), cols), F32),
-            jax.ShapeDtypeStruct((OPS * TAPS, rows, cols), F32),
+            jax.ShapeDtypeStruct((2, (count + SUB) * (rows + 1), cols), F32),
+            jax.ShapeDtypeStruct((OPS * TAPS, rows + 2 * SUB, cols), F32),
         ),
         in_specs=[smem, hbm, hbm, hbm, hbm],
         out_specs=(vmem,) * 6,
@@ -360,9 +360,9 @@
             pltpu.SMEM((OPS, RANGE), F32),
             VMEM((2, count, rows, cols), BF16),
             VMEM((OPS, TAPS, rows, cols), jnp.int32),
-            VMEM((2 * SUB * (rows + 1), cols), F32),
-            VMEM((edge_rows * SUB, cols), F32),
-            VMEM((edge_rows * SUB, cols), F32),
+            VMEM((3 * SUB * (rows + 1), cols), F32),
+            VMEM((edge_rows * SUB + SUB, cols), F32),
+            VMEM((edge_rows * SUB + SUB, cols), F32),
             pltpu.SemaphoreType.DMA((2 * (count // (2 * SUB)) + OPS + 1,)),
         ],
         compiler_params=params,
@@ -399,7 +399,7 @@
         in_specs=[smem, smem] + [vmem] * 8,
         out_specs=vmem,
         scratch_shapes=[
-            VMEM((2, len(ODD), tiles, count, cols), F32),
+            VMEM((2, len(ODD), tiles, count, cols), BF16),
             VMEM((len(EVEN) * TAPS, RANGE, cols), F32),
             VMEM((2, 2 * RANGE, len(EVEN) * count, cols), BF16),
             VMEM((size, size), F32),

time: 34 us -> 32.4 us (0.953)
  Pallas kernels: 15.8 us -> 14.2 us
    pallas_call x1, Pallas kernels: 4.93 us -> 4.1 us  [on_device(): pl.pallas_call(lambda *refs: main_kernel((wide, narrow), *refs), out_shap...]
    pallas_call x1, Pallas kernels: 7.47 us -> 6.72 us  [on_device(): pl.pallas_call(inner_kernel, out_shape=(jax.ShapeDtypeStruct((2, rows, le...]
  transfers between devices with their start and end apart: 3 -> 3, of which waited for: 0 -> 0; matrix products, arithmetic and copies ran while one was open for 0% -> 0% of each run, Pallas kernels for 22% -> 21%
where the time goes in v6:
time: 32.4 us; the launch traced here: 32.2 us
  Pallas kernels  14.2 us (44%)
  blocking collectives  10.3 us (32%)
  starting transfers between devices  7.7 us (24%)
    all_to_all x1, blocking collectives, on_device(): got = lax.all_to_all(partial, ('wide', 'narrow'), 0, 0, tiled=True)  10.3 us
    ppermute x3, starting transfers between devices, swap(): return lax.ppermute(array, axis, pairs)  7.7 us
    pallas_call x1, Pallas kernels, on_device(): pl.pallas_call(inner_kernel, out_shape=(jax.ShapeDtypeStruct((2, rows, le...  6.72 us
    pallas_call x1, Pallas kernels, on_device(): pl.pallas_call(lambda *refs: main_kernel((wide, narrow), *refs), out_shap...  4.1 us
    pallas_call x1, Pallas kernels, on_device(): pl.pallas_call(pack_kernel, out_shape=(jax.ShapeDtypeStruct((RANGE, edge_...  2.61 us
    pallas_call x1, Pallas kernels, on_device(): pl.pallas_call(lambda *refs: sum_kernel(factor, *refs), out_shape=jax.Sha...  0.72 us
  transfers between devices with their start and end apart: 3, of which 0 were waited for; matrix products, arithmetic and copies ran while one was open for 0% of the time, Pallas kernels for 21%

profile of v6, /device:TPU:0, one launch (start us, length us, event | category | flops | bytes accessed | tf_op | source)
XLA Modules:
  0.0 32.2 jit_solution(5707959582592490550)
XLA Ops:
  0.0 0.0 copy-start
  0.0 2.6 %pack.1 = (bf16[4,144,128]{2,1,0:T(8,128)(2,1)S(1)}, bf16[4,144,128]{2,1,0:T(8,128)(2,1)S(1)}, bf16[4,144,128]{2,1,0:T(8,128)(2,1)S(1)}, bf16[4,16,128]{2,1,0:T(...) custom-call(s32[1]{0:T(128)} %bitcast.parity.refs_0_, f32[4,4]{1,0:T(4,128)} %refs_1_.1, ...), custom_call_target="tpu_custom_call" | custom-call | tf_op jit(solution)/shard_map/pack/pallas_call | solution.py:347
  2.6 0.6 %collective-permute-start = (bf16[4,144,128]{2,1,0:T(8,128)(2,1)S(1)}, bf16[4,144,128]{2,1,0:T(8,128)(2,1)S(1)}, u32[]{:S(2)}, u32[]{:S(2)}) collective-permute-start(bf16[4,144,128]{2,1,0:T(8,128)(2,1)S(1)} %get-tuple-element.17), channel_id=1, source_target_pairs={{0,2},{2,0},{4,6},{6,4},{8,10},{10,8},{12,14},{14,12},{16,18},{18,... | collective-permute-start | bytes 442376 | tf_op jit(solution)/shard_map/ppermute | solution.py:331
  3.2 5.7 %collective-permute-start.1 = (bf16[4,144,128]{2,1,0:T(8,128)(2,1)S(1)}, bf16[4,144,128]{2,1,0:T(8,128)(2,1)S(1)}, u32[]{:S(2)}, u32[]{:S(2)}) collective-permute-start(bf16[4,144,128]{2,1,0:T(8,128)(2,1)S(1)} %get-tuple-element.18), channel_id=1, source_target_pairs={{0,30},{2,4},{4,2},{6,8},{8,6},{10,12},{12,10},{14,16},{16,14},{18... | collective-permute-start | bytes 442376 | tf_op jit(solution)/shard_map/ppermute | solution.py:331
  8.8 1.5 %collective-permute-start.2 = (bf16[4,144,128]{2,1,0:T(8,128)(2,1)S(1)}, bf16[4,144,128]{2,1,0:T(8,128)(2,1)S(1)}, u32[]{:S(2)}, u32[]{:S(2)}) collective-permute-start(bf16[4,144,128]{2,1,0:T(8,128)(2,1)S(1)} %get-tuple-element.19), channel_id=1, source_target_pairs={{0,1},{1,0},{2,3},{3,2},{4,5},{5,4},{6,7},{7,6},{8,9},{9,8},{10,11... | collective-permute-start | bytes 442376 | tf_op jit(solution)/shard_map/ppermute | solution.py:331
  10.3 6.7 %interior.1 = (bf16[2,64,128,128]{3,2,1,0:T(8,128)(2,1)S(1)}, f32[2,64,64,256]{3,2,1,0:T(8,128)S(1)}) custom-call(f32[2,4680,128]{2,1,0:T(8,128)S(1)} %get-tuple-element.14.value.refs_3_, f32[32,80,128]{2,1,0:T(8,128)S(1)} %get-tuple-element.13.coef.refs_2_), custom_call_target="tpu_custom_call" | custom-call | tf_op jit(solution)/shard_map/interior/pallas_call | solution.py:371
  17.1 0.0 collective-permute-done.refs_6_
  17.1 0.0 collective-permute-done.1.refs_7_
  17.1 0.0 collective-permute-done.2.refs_8_
  17.1 0.0 copy-done
  17.1 4.1 %moments.1 = bf16[32,16,128]{2,1,0:T(8,128)(2,1)S(1)} custom-call(s32[1]{0:T(128)} %bitcast.parity.refs_0_, f32[4,4]{1,0:T(4,128)S(1)} %copy-done, f32[32,80,128]{2,1,0:T(8,128)S(1)} %get-tuple-element.13.coef.refs_2_, f32[2,4680,128]{2,1,0:T(8,128)S(1)} %get-tuple-element.14.value.refs_3_, bf16[2,64,128,128]{3,2,1,0:T(8,128)(2,1)S(1)} %get-tuple-element.15.refs_4_, ...), custom_call_target="tpu_custom_call" | custom-call | tf_op jit(solution)/shard_map/moments/pallas_call | solution.py:396
  21.2 10.3 %all_to_all.5.refs_0_ = bf16[32,16,128]{2,1,0:T(8,128)(2,1)S(1)} all-to-all(bf16[32,16,128]{2,1,0:T(8,128)(2,1)S(1)} %moments.1), channel_id=1, replica_groups=mesh['wide'=16,'narrow'=2] {'wide','narrow'}, dimensions={0} | all-to-all | bytes 262144 | tf_op jit(solution)/shard_map/all_to_all | solution.py:412
  31.5 0.7 %total.1 = f32[16,4,32]{2,1,0:T(4,128)} custom-call(bf16[32,16,128]{2,1,0:T(8,128)(2,1)S(1)} %all_to_all.5.refs_0_), custom_call_target="tpu_custom_call" | custom-call | tf_op jit(solution)/shard_map/total/pallas_call | solution.py:414
Async XLA Ops:
  0.0 17.1 %copy-start = (f32[4,4]{1,0:T(4,128)S(1)}, f32[4,4]{1,0:T(4,128)}, u32[]{:S(2)}) copy-start(f32[4,4]{1,0:T(4,128)} %refs_1_.1) | copy-start | bytes 196
  2.6 14.4 %collective-permute-start = (bf16[4,144,128]{2,1,0:T(8,128)(2,1)S(1)}, bf16[4,144,128]{2,1,0:T(8,128)(2,1)S(1)}, u32[]{:S(2)}, u32[]{:S(2)}) collective-permute-start(bf16[4,144,128]{2,1,0:T(8,128)(2,1)S(1)} %get-tuple-element.17), channel_id=1, source_target_pairs={{0,2},{2,0},{4,6},{6,4},{8,10},{10,8},{12,14},{14,12},{16,18},{18,... | collective-permute-start | bytes 442376 | tf_op jit(solution)/shard_map/ppermute | solution.py:331
  3.2 13.9 %collective-permute-start.1 = (bf16[4,144,128]{2,1,0:T(8,128)(2,1)S(1)}, bf16[4,144,128]{2,1,0:T(8,128)(2,1)S(1)}, u32[]{:S(2)}, u32[]{:S(2)}) collective-permute-start(bf16[4,144,128]{2,1,0:T(8,128)(2,1)S(1)} %get-tuple-element.18), channel_id=1, source_target_pairs={{0,30},{2,4},{4,2},{6,8},{8,6},{10,12},{12,10},{14,16},{16,14},{18... | collective-permute-start | bytes 442376 | tf_op jit(solution)/shard_map/ppermute | solution.py:331
  8.8 8.2 %collective-permute-start.2 = (bf16[4,144,128]{2,1,0:T(8,128)(2,1)S(1)}, bf16[4,144,128]{2,1,0:T(8,128)(2,1)S(1)}, u32[]{:S(2)}, u32[]{:S(2)}) collective-permute-start(bf16[4,144,128]{2,1,0:T(8,128)(2,1)S(1)} %get-tuple-element.19), channel_id=1, source_target_pairs={{0,1},{1,0},{2,3},{3,2},{4,5},{5,4},{6,7},{7,6},{8,9},{9,8},{10,11... | collective-permute-start | bytes 442376 | tf_op jit(solution)/shard_map/ppermute | solution.py:331

commit v7 on v6

--- a/solution.py
+++ b/solution.py
@@ -20,7 +20,6 @@
 BF16 = jnp.bfloat16
 INNER_BODY = 28
 INNER_LEAD = 6
-MAIN_BODY = 28
 VMEM_LIMIT = 24 * 1024 * 1024
 
 
@@ -28,7 +27,7 @@
     return lax.broadcasted_iota(jnp.int32, shape, len(shape) - 1)
 
 
-def pack_kernel(parity, hop_far, right, left, bonds, near, far, side, own, value, coef, hop, vectors, bits, flat, head, tail, sems):
+def pack_kernel(widths, parity, hop_far, right, left, bonds, near, far, side, own, value, coef, orders, hop, vectors, bits, flat, head, tail, sems):
     count, rows, cols = right.shape
     even = parity[0] == 0
     group = LANES // TAPS
@@ -46,6 +45,18 @@
     copies = [pltpu.make_async_copy(src, dst, sems.at[n]) for n, (src, dst) in enumerate(copies)]
     for copy in copies:
         copy.start()
+
+    size = OPS * count
+
+    def order(parts, dim):
+        per = count // parts
+        new = lax.broadcasted_iota(jnp.int32, (size, size), dim)
+        old = lax.broadcasted_iota(jnp.int32, (size, size), 1 - dim)
+        part, rest = new // (OPS * per), new % (OPS * per)
+        return jnp.where(old == (rest // per) * count + part * per + rest % per, 1.0, 0.0).astype(BF16)
+
+    for dim in range(2):
+        orders[dim] = order(widths[dim], dim)
 
     lane = lane_index((batch, cols)) // TAPS
 
@@ -185,7 +196,7 @@
             lines(RANGE + step * INNER_BODY + n)
 
 
-def main_kernel(widths, parity, hop, coef, value, inner, along, near, far, side, own, out, band, near_ends, ends, acc):
+def main_kernel(widths, parity, hop, coef, value, inner, along, near, far, side, own, orders, out, band, beyond_rows, near_ends, ends, acc):
     _, rows, count, _ = along.shape
     cols = coef.shape[2]
     pitch = rows + 1
@@ -195,10 +206,11 @@
     def scale_of(a, index):
         return hop[a, index % RANGE] * (1.0 if index < RANGE else -1.0)
 
+    beyond_rows[0] = jnp.where(even, far[...], near[...])
+    beyond_rows[1] = jnp.where(even, near[...], far[...])
+
     def outer(slab, row):
-        low = jnp.where(even, far[row, slab, :].astype(F32), near[row, slab, :].astype(F32))
-        high = jnp.where(even, near[row, slab, :].astype(F32), far[row, slab, :].astype(F32))
-        return low, high
+        return [beyond_rows[end, row, slab, :].astype(F32) for end in range(2)]
 
     for row in range(RANGE):
         low, high = outer(slice(2 * count, 2 * count + 2 * SUB), row)
@@ -207,34 +219,34 @@
             source = low if index < RANGE else high
             near_ends[slot, row : row + 1, :] = source[slot : slot + 1] * scale_of(a, index)
 
-    for end in range(2):
-        for n in range(RANGE):
-            row = n if end == 0 else rows - RANGE + n
-            for which in range(2):
-                def value_at(step, base):
-                    at = row + step
-                    slab = slice(which * count + base, which * count + base + 2 * SUB)
-                    if at < 0:
-                        return outer(slab, at + RANGE)[0]
-                    if at >= rows:
-                        return outer(slab, at - rows)[1]
-                    parts = [value[which, pl.ds((base + half * SUB) * pitch + at, SUB, stride=pitch), :] for half in range(2)]
-                    return jnp.concatenate(parts, axis=0)
-
-                def factor_at(a, index):
-                    at = factor_row(which, row, index)
-                    if 0 <= at < rows:
-                        one = coef[a * TAPS + index, at : at + 1, :]
-                    else:
-                        at = at + RANGE if at < 0 else at - rows
-                        one = near_ends[EVEN.index(a) * TAPS + index, at : at + 1, :]
-                    return jnp.broadcast_to(one, (2 * SUB, cols))
-
-                for base in range(0, count, 2 * SUB):
-                    totals = along_rows(which, lambda step, base=base: value_at(step, base), factor_at)
-                    for o, a in enumerate(EVEN):
-                        at = o * count + base
-                        ends[which, end * RANGE + n, at : at + 2 * SUB, :] = totals[a].astype(BF16)
+    def end_piece(end, n, which, base):
+        row = n if end == 0 else rows - RANGE + n
+        slab = slice(which * count + base, which * count + base + 2 * SUB)
+
+        def value_at(step):
+            at = row + step
+            if at < 0:
+                return outer(slab, at + RANGE)[0]
+            if at >= rows:
+                return outer(slab, at - rows)[1]
+            parts = [value[which, pl.ds((base + half * SUB) * pitch + at, SUB, stride=pitch), :] for half in range(2)]
+            return jnp.concatenate(parts, axis=0)
+
+        def factor_at(a, index):
+            at = factor_row(which, row, index)
+            if 0 <= at < rows:
+                return coef[a * TAPS + index, pl.ds(at, 2 * SUB, stride=0), :]
+            at = at + RANGE if at < 0 else at - rows
+            return near_ends[EVEN.index(a) * TAPS + index, pl.ds(at, 2 * SUB, stride=0), :]
+
+        totals = along_rows(which, value_at, factor_at)
+        for o, a in enumerate(EVEN):
+            at = o * count + base
+            ends[which, end * RANGE + n, at : at + 2 * SUB, :] = totals[a].astype(BF16)
+
+    pieces = [
+        (end, n, which, base) for end in range(2) for n in range(RANGE) for which in range(2) for base in range(0, count, 2 * SUB)
+    ]
 
     tile_shape = (count, cols)
     spot = lane_index((1, cols)) % TAPS
@@ -246,7 +258,7 @@
             packed = side[tile, which * count : (which + 1) * count, :]
             total = {}
             for k in range(1, RANGE + 1):
-                moved = jnp.where(spots < RANGE, pltpu.roll(packed, LANES - k, 1).astype(F32), pltpu.roll(packed, k, 1).astype(F32))
+                moved = jnp.where(spots < RANGE, pltpu.roll(packed, LANES - k, 1), pltpu.roll(packed, k, 1)).astype(F32)
                 for a in ODD:
                     slot = ODD.index(a) * TAPS + k - 1
                     if which == 0:
@@ -264,6 +276,7 @@
 
     acc[...] = jnp.zeros_like(acc)
     rim_lane = (lane_index(tile_shape) < RANGE) | (lane_index(tile_shape) >= cols - RANGE)
+    rim = jnp.where(rim_lane, 1.0, 0.0).astype(BF16)
 
     def results(row, even_of):
         found = []
@@ -273,43 +286,35 @@
             both = along[which, row]
             done = {a: even_of(which)[EVEN.index(a) * count : (EVEN.index(a) + 1) * count] for a in EVEN}
             for o, a in enumerate(ODD):
-                beyond = jnp.where(rim_lane, pltpu.roll(band[which, o, tile], turn, 1).astype(F32), 0.0)
+                beyond = (pltpu.roll(band[which, o, tile], turn, 1) * rim).astype(F32)
                 done[a] = (both[:, o * cols : (o + 1) * cols] + beyond).astype(BF16)
             found.append(jnp.concatenate([done[a] for a in range(OPS)], axis=0))
         return found
 
-    def accumulate(pairs):
-        for pair in pairs:
-            found = [results(*one) for one in pair]
-            first = jnp.concatenate([one[0] for one in found], axis=1)
-            back = jnp.concatenate([one[1] for one in found], axis=1)
-            acc[...] += lax.dot_general(back, first, (((1,), (1,)), ((), ())), preferred_element_type=F32)
+    def accumulate(pair):
+        found = [results(*one) for one in pair]
+        first = jnp.concatenate([one[0] for one in found], axis=1)
+        back = jnp.concatenate([one[1] for one in found], axis=1)
+        acc[...] += lax.dot_general(back, first, (((1,), (1,)), ((), ())), preferred_element_type=F32)
 
     def end_row(n):
         return (n if n < RANGE else rows - 2 * RANGE + n), lambda which: ends[which, n]
 
-    accumulate([[end_row(n), end_row(n + 1)] for n in range(0, 2 * RANGE, 2)])
-
-    @pl.loop(0, (rows - 2 * RANGE) // MAIN_BODY)
-    def _(step):
-        def inner_row(n):
-            row = RANGE + step * MAIN_BODY + n
-            return row, lambda which: inner[which, row]
-
-        accumulate([[inner_row(n), inner_row(n + 1)] for n in range(0, MAIN_BODY, 2)])
+    def inner_row(row):
+        return row, lambda which: inner[which, row]
+
+    middle_rows = range(RANGE, rows - RANGE, 2)
+    for n, row in enumerate(middle_rows):
+        for piece in pieces[n * len(pieces) // len(middle_rows) : (n + 1) * len(pieces) // len(middle_rows)]:
+            end_piece(*piece)
+        accumulate([inner_row(row), inner_row(row + 1)])
+    for n in range(0, 2 * RANGE, 2):
+        accumulate([end_row(n), end_row(n + 1)])
 
     parts_left, parts_right = widths
     per_left, per_right = count // parts_left, count // parts_right
-    size = OPS * count
-
-    def order(per, dim):
-        new = lax.broadcasted_iota(jnp.int32, (size, size), dim)
-        old = lax.broadcasted_iota(jnp.int32, (size, size), 1 - dim)
-        part, rest = new // (OPS * per), new % (OPS * per)
-        return jnp.where(old == (rest // per) * count + part * per + rest % per, 1.0, 0.0).astype(BF16)
-
-    moved = jnp.dot(order(per_left, 0), acc[...].astype(BF16), preferred_element_type=F32).astype(BF16)
-    moved = jnp.dot(moved, order(per_right, 1), preferred_element_type=F32).astype(BF16)
+    moved = jnp.dot(orders[0], acc[...].astype(BF16), preferred_element_type=F32).astype(BF16)
+    moved = jnp.dot(moved, orders[1], preferred_element_type=F32).astype(BF16)
     if out.ndim == 2:
         out[...] = moved
     else:
@@ -344,8 +349,8 @@
 
     hbm = pl.BlockSpec(memory_space=pltpu.HBM)
 
-    near, far, side, own, value, coef = pl.pallas_call(
-        pack_kernel,
+    near, far, side, own, value, coef, orders = pl.pallas_call(
+        lambda *refs: pack_kernel((wide, narrow), *refs),
         out_shape=(
             jax.ShapeDtypeStruct((RANGE, edge_rows, cols), BF16),
             jax.ShapeDtypeStruct((RANGE, edge_rows, cols), BF16),
@@ -353,9 +358,10 @@
             jax.ShapeDtypeStruct((tiles, side_rows - 2 * count, cols), BF16),
             jax.ShapeDtypeStruct((2, (count + SUB) * (rows + 1), cols), F32),
             jax.ShapeDtypeStruct((OPS * TAPS, rows + 2 * SUB, cols), F32),
+            jax.ShapeDtypeStruct((2, OPS * count, OPS * count), BF16),
         ),
         in_specs=[smem, hbm, hbm, hbm, hbm],
-        out_specs=(vmem,) * 6,
+        out_specs=(vmem,) * 7,
         scratch_shapes=[
             pltpu.SMEM((OPS, RANGE), F32),
             VMEM((2, count, rows, cols), BF16),
@@ -396,17 +402,18 @@
     partial = pl.pallas_call(
         lambda *refs: main_kernel((wide, narrow), *refs),
         out_shape=jax.ShapeDtypeStruct(blocked if direct else (size, size), BF16),
-        in_specs=[smem, smem] + [vmem] * 8,
+        in_specs=[smem, smem] + [vmem] * 9,
         out_specs=vmem,
         scratch_shapes=[
             VMEM((2, len(ODD), tiles, count, cols), BF16),
-            VMEM((len(EVEN) * TAPS, RANGE, cols), F32),
+            VMEM((2, RANGE, edge_rows, cols), BF16),
+            VMEM((len(EVEN) * TAPS, RANGE + 2 * SUB, cols), F32),
             VMEM((2, 2 * RANGE, len(EVEN) * count, cols), BF16),
             VMEM((size, size), F32),
         ],
         compiler_params=params,
         name="moments",
-    )(parity, hop, coef, value, inner, along, near, far, side, own)
+    )(parity, hop, coef, value, inner, along, near, far, side, own, orders)
     if not direct:
         partial = partial.reshape(wide, OPS * per_left, narrow, OPS * per_right).transpose(0, 2, 1, 3).reshape(blocked)
     got = lax.all_to_all(partial, ("wide", "narrow"), 0, 0, tiled=True)

time: 32.4 us -> 32.1 us (level)
  Pallas kernels: 14.2 us -> 13.8 us
    pallas_call x1, Pallas kernels: 4.1 us -> 3.76 us  [on_device(): pl.pallas_call(lambda *refs: main_kernel((wide, narrow), *refs), out_shap...]
where the time goes in v7:
time: 32.1 us; the launch traced here: 31.9 us
  Pallas kernels  13.8 us (43%)
  blocking collectives  10.3 us (32%)
  starting transfers between devices  7.7 us (24%)
    all_to_all x1, blocking collectives, on_device(): got = lax.all_to_all(partial, ('wide', 'narrow'), 0, 0, tiled=True)  10.3 us
    ppermute x3, starting transfers between devices, swap(): return lax.ppermute(array, axis, pairs)  7.7 us
    pallas_call x1, Pallas kernels, on_device(): pl.pallas_call(inner_kernel, out_shape=(jax.ShapeDtypeStruct((2, rows, le...  6.72 us
    pallas_call x1, Pallas kernels, on_device(): pl.pallas_call(lambda *refs: main_kernel((wide, narrow), *refs), out_shap...  3.76 us
    pallas_call x1, Pallas kernels, on_device(): pl.pallas_call(lambda *refs: pack_kernel((wide, narrow), *refs), out_shap...  2.61 us
    pallas_call x1, Pallas kernels, on_device(): pl.pallas_call(lambda *refs: sum_kernel(factor, *refs), out_shape=jax.Sha...  0.72 us
  transfers between devices with their start and end apart: 3, of which 0 were waited for; matrix products, arithmetic and copies ran while one was open for 0% of the time, Pallas kernels for 21%

profile of v7, /device:TPU:0, one launch (start us, length us, event | category | flops | bytes accessed | tf_op | source)
XLA Modules:
  0.0 31.9 jit_solution(13950426533862718848)
XLA Ops:
  0.0 0.0 copy-start
  0.0 2.6 %pack.1 = (bf16[4,144,128]{2,1,0:T(8,128)(2,1)S(1)}, bf16[4,144,128]{2,1,0:T(8,128)(2,1)S(1)}, bf16[4,144,128]{2,1,0:T(8,128)(2,1)S(1)}, bf16[4,16,128]{2,1,0:T(...) custom-call(s32[1]{0:T(128)} %bitcast.refs_0_, ...), custom_call_target="tpu_custom_call" | custom-call | tf_op jit(solution)/shard_map/pack/pallas_call | solution.py:352
  2.6 0.6 %collective-permute-start = (bf16[4,144,128]{2,1,0:T(8,128)(2,1)S(1)}, bf16[4,144,128]{2,1,0:T(8,128)(2,1)S(1)}, u32[]{:S(2)}, u32[]{:S(2)}) collective-permute-start(bf16[4,144,128]{2,1,0:T(8,128)(2,1)S(1)} %get-tuple-element.18), channel_id=1, source_target_pairs={{0,2},{2,0},{4,6},{6,4},{8,10},{10,8},{12,14},{14,12},{16,18},{18,... | collective-permute-start | bytes 442376 | tf_op jit(solution)/shard_map/ppermute | solution.py:336
  3.2 5.7 %collective-permute-start.1 = (bf16[4,144,128]{2,1,0:T(8,128)(2,1)S(1)}, bf16[4,144,128]{2,1,0:T(8,128)(2,1)S(1)}, u32[]{:S(2)}, u32[]{:S(2)}) collective-permute-start(bf16[4,144,128]{2,1,0:T(8,128)(2,1)S(1)} %get-tuple-element.19), channel_id=1, source_target_pairs={{0,30},{2,4},{4,2},{6,8},{8,6},{10,12},{12,10},{14,16},{16,14},{18... | collective-permute-start | bytes 442376 | tf_op jit(solution)/shard_map/ppermute | solution.py:336
  8.8 1.5 %collective-permute-start.2 = (bf16[4,144,128]{2,1,0:T(8,128)(2,1)S(1)}, bf16[4,144,128]{2,1,0:T(8,128)(2,1)S(1)}, u32[]{:S(2)}, u32[]{:S(2)}) collective-permute-start(bf16[4,144,128]{2,1,0:T(8,128)(2,1)S(1)} %get-tuple-element.20), channel_id=1, source_target_pairs={{0,1},{1,0},{2,3},{3,2},{4,5},{5,4},{6,7},{7,6},{8,9},{9,8},{10,11... | collective-permute-start | bytes 442376 | tf_op jit(solution)/shard_map/ppermute | solution.py:336
  10.3 6.7 %interior.1 = (bf16[2,64,128,128]{3,2,1,0:T(8,128)(2,1)S(1)}, f32[2,64,64,256]{3,2,1,0:T(8,128)S(1)}) custom-call(f32[2,4680,128]{2,1,0:T(8,128)S(1)} %get-tuple-element.15.value.refs_3_, f32[32,80,128]{2,1,0:T(8,128)S(1)} %get-tuple-element.14.coef.refs_2_), custom_call_target="tpu_custom_call" | custom-call | tf_op jit(solution)/shard_map/interior/pallas_call | solution.py:377
  17.1 0.0 collective-permute-done.refs_6_
  17.1 0.0 collective-permute-done.1.refs_7_
  17.1 0.0 collective-permute-done.2.refs_8_
  17.1 0.0 copy-done
  17.1 3.8 %moments.1 = bf16[32,16,128]{2,1,0:T(8,128)(2,1)S(1)} custom-call(s32[1]{0:T(128)} %bitcast.refs_0_, f32[4,4]{1,0:T(4,128)S(1)} %copy-done, f32[32,80,128]{2,1,0:T(8,128)S(1)} %get-tuple-element.14.coef.refs_2_, f32[2,4680,128]{2,1,0:T(8,128)S(1)} %get-tuple-element.15.value.refs_3_, bf16[2,64,128,128]{3,2,1,0:T(8,128)(2,1)S(1)} %get-tuple-element.16.refs_4_, ...), custom_call_target="tpu_custom_call" | custom-call | tf_op jit(solution)/shard_map/moments/pallas_call | solution.py:402
  20.9 10.3 %all_to_all.5.refs_0_ = bf16[32,16,128]{2,1,0:T(8,128)(2,1)S(1)} all-to-all(bf16[32,16,128]{2,1,0:T(8,128)(2,1)S(1)} %moments.1), channel_id=1, replica_groups=mesh['wide'=16,'narrow'=2] {'wide','narrow'}, dimensions={0} | all-to-all | bytes 262144 | tf_op jit(solution)/shard_map/all_to_all | solution.py:419
  31.2 0.7 %total.1 = f32[16,4,32]{2,1,0:T(4,128)} custom-call(bf16[32,16,128]{2,1,0:T(8,128)(2,1)S(1)} %all_to_all.5.refs_0_), custom_call_target="tpu_custom_call" | custom-call | tf_op jit(solution)/shard_map/total/pallas_call | solution.py:421
Async XLA Ops:
  0.0 17.1 %copy-start = (f32[4,4]{1,0:T(4,128)S(1)}, f32[4,4]{1,0:T(4,128)}, u32[]{:S(2)}) copy-start(f32[4,4]{1,0:T(4,128)} %refs_1_.3) | copy-start | bytes 196
  2.6 14.4 %collective-permute-start = (bf16[4,144,128]{2,1,0:T(8,128)(2,1)S(1)}, bf16[4,144,128]{2,1,0:T(8,128)(2,1)S(1)}, u32[]{:S(2)}, u32[]{:S(2)}) collective-permute-start(bf16[4,144,128]{2,1,0:T(8,128)(2,1)S(1)} %get-tuple-element.18), channel_id=1, source_target_pairs={{0,2},{2,0},{4,6},{6,4},{8,10},{10,8},{12,14},{14,12},{16,18},{18,... | collective-permute-start | bytes 442376 | tf_op jit(solution)/shard_map/ppermute | solution.py:336
  3.2 13.9 %collective-permute-start.1 = (bf16[4,144,128]{2,1,0:T(8,128)(2,1)S(1)}, bf16[4,144,128]{2,1,0:T(8,128)(2,1)S(1)}, u32[]{:S(2)}, u32[]{:S(2)}) collective-permute-start(bf16[4,144,128]{2,1,0:T(8,128)(2,1)S(1)} %get-tuple-element.19), channel_id=1, source_target_pairs={{0,30},{2,4},{4,2},{6,8},{8,6},{10,12},{12,10},{14,16},{16,14},{18... | collective-permute-start | bytes 442376 | tf_op jit(solution)/shard_map/ppermute | solution.py:336
  8.8 8.2 %collective-permute-start.2 = (bf16[4,144,128]{2,1,0:T(8,128)(2,1)S(1)}, bf16[4,144,128]{2,1,0:T(8,128)(2,1)S(1)}, u32[]{:S(2)}, u32[]{:S(2)}) collective-permute-start(bf16[4,144,128]{2,1,0:T(8,128)(2,1)S(1)} %get-tuple-element.20), channel_id=1, source_target_pairs={{0,1},{1,0},{2,3},{3,2},{4,5},{5,4},{6,7},{7,6},{8,9},{9,8},{10,11... | collective-permute-start | bytes 442376 | tf_op jit(solution)/shard_map/ppermute | solution.py:336

commit v8 on v7

--- a/solution.py
+++ b/solution.py
@@ -43,7 +43,7 @@
         copies.append((bonds.at[a], bits.at[a]))
     copies.append((hop_far, hop))
     copies = [pltpu.make_async_copy(src, dst, sems.at[n]) for n, (src, dst) in enumerate(copies)]
-    for copy in copies:
+    for copy in copies[:batches] + copies[2 * batches :] + copies[batches : 2 * batches]:
         copy.start()
 
     size = OPS * count
@@ -82,9 +82,9 @@
             near[row, at : at + batch, :] = jnp.where(even, high, low).astype(BF16)
             far[row, at : at + batch, :] = jnp.where(even, low, high).astype(BF16)
 
-    for which in range(2):
+    def vectors_of(which, together):
         for n in range(batches):
-            for m in range(n, n + 4 if n % 4 == 0 else n):
+            for m in range(n, n + together if n % together == 0 else n):
                 copies[which * batches + m].wait()
             at = which * count + n * batch
             for v in range(batch):
@@ -95,6 +95,8 @@
                 tail[(at + v) * SUB : (at + v + 1) * SUB, :] = one[rows - SUB :]
             pack(at, value.at[which, pl.ds(n * batch * pitch, (batch + SUB) * pitch)])
             send(at)
+
+    vectors_of(0, batches)
     at = 2 * count
     copies[-1].wait()
     for n, a in enumerate(ODD + EVEN):
@@ -112,6 +114,7 @@
                 tail[t * SUB : (t + 1) * SUB, :] = sign[rows - SUB :]
     pack(at, flat)
     send(at)
+    vectors_of(1, batches)
     own[...] = side[:, at:, :]
 
 

time: 32.1 us -> 32 us (level)
  no operation moved by 1% of the time
where the time goes in v8:
time: 32 us; the launch traced here: 31.9 us
  Pallas kernels  13.8 us (43%)
  blocking collectives  10.3 us (32%)
  starting transfers between devices  7.7 us (24%)
    all_to_all x1, blocking collectives, on_device(): got = lax.all_to_all(partial, ('wide', 'narrow'), 0, 0, tiled=True)  10.3 us
    ppermute x3, starting transfers between devices, swap(): return lax.ppermute(array, axis, pairs)  7.7 us
    pallas_call x1, Pallas kernels, on_device(): pl.pallas_call(inner_kernel, out_shape=(jax.ShapeDtypeStruct((2, rows, le...  6.72 us
    pallas_call x1, Pallas kernels, on_device(): pl.pallas_call(lambda *refs: main_kernel((wide, narrow), *refs), out_shap...  3.76 us
    pallas_call x1, Pallas kernels, on_device(): pl.pallas_call(lambda *refs: pack_kernel((wide, narrow), *refs), out_shap...  2.6 us
    pallas_call x1, Pallas kernels, on_device(): pl.pallas_call(lambda *refs: sum_kernel(factor, *refs), out_shape=jax.Sha...  0.72 us
  transfers between devices with their start and end apart: 3, of which 0 were waited for; matrix products, arithmetic and copies ran while one was open for 0% of the time, Pallas kernels for 21%

profile of v8, /device:TPU:0, one launch (start us, length us, event | category | flops | bytes accessed | tf_op | source)
XLA Modules:
  0.0 31.9 jit_solution(13612107633464317247)
XLA Ops:
  0.0 0.0 copy-start
  0.0 2.6 %pack.1 = (bf16[4,144,128]{2,1,0:T(8,128)(2,1)S(1)}, bf16[4,144,128]{2,1,0:T(8,128)(2,1)S(1)}, bf16[4,144,128]{2,1,0:T(8,128)(2,1)S(1)}, bf16[4,16,128]{2,1,0:T(...) custom-call(s32[1]{0:T(128)} %bitcast.refs_0_, ...), custom_call_target="tpu_custom_call" | custom-call | tf_op jit(solution)/shard_map/pack/pallas_call | solution.py:355
  2.6 0.6 %collective-permute-start = (bf16[4,144,128]{2,1,0:T(8,128)(2,1)S(1)}, bf16[4,144,128]{2,1,0:T(8,128)(2,1)S(1)}, u32[]{:S(2)}, u32[]{:S(2)}) collective-permute-start(bf16[4,144,128]{2,1,0:T(8,128)(2,1)S(1)} %get-tuple-element.18), channel_id=1, source_target_pairs={{0,2},{2,0},{4,6},{6,4},{8,10},{10,8},{12,14},{14,12},{16,18},{18,... | collective-permute-start | bytes 442376 | tf_op jit(solution)/shard_map/ppermute | solution.py:339
  3.2 5.7 %collective-permute-start.1 = (bf16[4,144,128]{2,1,0:T(8,128)(2,1)S(1)}, bf16[4,144,128]{2,1,0:T(8,128)(2,1)S(1)}, u32[]{:S(2)}, u32[]{:S(2)}) collective-permute-start(bf16[4,144,128]{2,1,0:T(8,128)(2,1)S(1)} %get-tuple-element.19), channel_id=1, source_target_pairs={{0,30},{2,4},{4,2},{6,8},{8,6},{10,12},{12,10},{14,16},{16,14},{18... | collective-permute-start | bytes 442376 | tf_op jit(solution)/shard_map/ppermute | solution.py:339
  8.8 1.5 %collective-permute-start.2 = (bf16[4,144,128]{2,1,0:T(8,128)(2,1)S(1)}, bf16[4,144,128]{2,1,0:T(8,128)(2,1)S(1)}, u32[]{:S(2)}, u32[]{:S(2)}) collective-permute-start(bf16[4,144,128]{2,1,0:T(8,128)(2,1)S(1)} %get-tuple-element.20), channel_id=1, source_target_pairs={{0,1},{1,0},{2,3},{3,2},{4,5},{5,4},{6,7},{7,6},{8,9},{9,8},{10,11... | collective-permute-start | bytes 442376 | tf_op jit(solution)/shard_map/ppermute | solution.py:339
  10.3 6.7 %interior.1 = (bf16[2,64,128,128]{3,2,1,0:T(8,128)(2,1)S(1)}, f32[2,64,64,256]{3,2,1,0:T(8,128)S(1)}) custom-call(f32[2,4680,128]{2,1,0:T(8,128)S(1)} %get-tuple-element.15.value.refs_3_, f32[32,80,128]{2,1,0:T(8,128)S(1)} %get-tuple-element.14.coef.refs_2_), custom_call_target="tpu_custom_call" | custom-call | tf_op jit(solution)/shard_map/interior/pallas_call | solution.py:380
  17.0 0.0 collective-permute-done.refs_6_
  17.1 0.0 collective-permute-done.1.refs_7_
  17.1 0.0 collective-permute-done.2.refs_8_
  17.1 0.0 copy-done
  17.1 3.8 %moments.1 = bf16[32,16,128]{2,1,0:T(8,128)(2,1)S(1)} custom-call(s32[1]{0:T(128)} %bitcast.refs_0_, f32[4,4]{1,0:T(4,128)S(1)} %copy-done, f32[32,80,128]{2,1,0:T(8,128)S(1)} %get-tuple-element.14.coef.refs_2_, f32[2,4680,128]{2,1,0:T(8,128)S(1)} %get-tuple-element.15.value.refs_3_, bf16[2,64,128,128]{3,2,1,0:T(8,128)(2,1)S(1)} %get-tuple-element.16.refs_4_, ...), custom_call_target="tpu_custom_call" | custom-call | tf_op jit(solution)/shard_map/moments/pallas_call | solution.py:405
  20.9 10.3 %all_to_all.5.refs_0_ = bf16[32,16,128]{2,1,0:T(8,128)(2,1)S(1)} all-to-all(bf16[32,16,128]{2,1,0:T(8,128)(2,1)S(1)} %moments.1), channel_id=1, replica_groups=mesh['wide'=16,'narrow'=2] {'wide','narrow'}, dimensions={0} | all-to-all | bytes 262144 | tf_op jit(solution)/shard_map/all_to_all | solution.py:422
  31.2 0.7 %total.1 = f32[16,4,32]{2,1,0:T(4,128)} custom-call(bf16[32,16,128]{2,1,0:T(8,128)(2,1)S(1)} %all_to_all.5.refs_0_), custom_call_target="tpu_custom_call" | custom-call | tf_op jit(solution)/shard_map/total/pallas_call | solution.py:424
Async XLA Ops:
  0.0 17.1 %copy-start = (f32[4,4]{1,0:T(4,128)S(1)}, f32[4,4]{1,0:T(4,128)}, u32[]{:S(2)}) copy-start(f32[4,4]{1,0:T(4,128)} %refs_1_.3) | copy-start | bytes 196
  2.6 14.4 %collective-permute-start = (bf16[4,144,128]{2,1,0:T(8,128)(2,1)S(1)}, bf16[4,144,128]{2,1,0:T(8,128)(2,1)S(1)}, u32[]{:S(2)}, u32[]{:S(2)}) collective-permute-start(bf16[4,144,128]{2,1,0:T(8,128)(2,1)S(1)} %get-tuple-element.18), channel_id=1, source_target_pairs={{0,2},{2,0},{4,6},{6,4},{8,10},{10,8},{12,14},{14,12},{16,18},{18,... | collective-permute-start | bytes 442376 | tf_op jit(solution)/shard_map/ppermute | solution.py:339
  3.2 13.9 %collective-permute-start.1 = (bf16[4,144,128]{2,1,0:T(8,128)(2,1)S(1)}, bf16[4,144,128]{2,1,0:T(8,128)(2,1)S(1)}, u32[]{:S(2)}, u32[]{:S(2)}) collective-permute-start(bf16[4,144,128]{2,1,0:T(8,128)(2,1)S(1)} %get-tuple-element.19), channel_id=1, source_target_pairs={{0,30},{2,4},{4,2},{6,8},{8,6},{10,12},{12,10},{14,16},{16,14},{18... | collective-permute-start | bytes 442376 | tf_op jit(solution)/shard_map/ppermute | solution.py:339
  8.8 8.2 %collective-permute-start.2 = (bf16[4,144,128]{2,1,0:T(8,128)(2,1)S(1)}, bf16[4,144,128]{2,1,0:T(8,128)(2,1)S(1)}, u32[]{:S(2)}, u32[]{:S(2)}) collective-permute-start(bf16[4,144,128]{2,1,0:T(8,128)(2,1)S(1)} %get-tuple-element.20), channel_id=1, source_target_pairs={{0,1},{1,0},{2,3},{3,2},{4,5},{5,4},{6,7},{7,6},{8,9},{9,8},{10,11... | collective-permute-start | bytes 442376 | tf_op jit(solution)/shard_map/ppermute | solution.py:339
